TPU v7x, 256 devices: a whole 4x4x8 slice. The times are simulated.
256 devices in a mesh: replica: 16 (over y_lo, x, core), shard: 16 (over y_hi, z).
Axes of the slice: x: 4, y: 4 (y_hi: 2, y_lo: 2; y = y_hi * 2 + y_lo), z: 8, core: 2. Of those that a mesh axis runs over, the one named last changes fastest.
Arguments:
- grads: bfloat16 [16, 16, 256, 8192], P('replica', 'shard'), may hold values from -1.25 to 1.25
- master: float32 [256, 8192], P('shard'), may hold values from -0.003 to 0.003
- moment_one: float32 [256, 8192], P('shard'), may hold values from -0.75 to 0.75
- moment_two: float32 [256, 8192], P('shard'), may hold values from 0.005 to 0.2
Outputs:
- master_out: float32 [256, 8192], P('shard')
- moment_one_out: float32 [256, 8192], P('shard')
- moment_two_out: float32 [256, 8192], P('shard')
- weights: bfloat16 [256, 8192], replicated
All inputs are finite; a program needn't handle non-finite values.
Results may differ from a plain program's by a relative error of at most 0.012.
Values may be sent and summed in bfloat16 or wider, within the bound.
No kernel may reach another device: no remote copies, remote signals or barrier semaphores. Data moves between devices by JAX's collectives and lax.ppermute only.
A program may use at most 64 MiB of HBM per device.

v0:
```python
import jax
import jax.numpy as jnp
from jax import lax
from jax.sharding import PartitionSpec as P

STEP = 20


def adam_update(total, master, moment_one, moment_two):
    first = 0.9 * moment_one + 0.1 * total
    second = 0.95 * moment_two + 0.05 * total * total
    first_hat = first / (1.0 - 0.9**STEP)
    second_hat = second / (1.0 - 0.95**STEP)
    updated = master - 0.0003 * (first_hat / (jnp.sqrt(second_hat) + 1e-08) + 0.1 * master)
    return (updated, first, second)


def local(grads, master, moment_one, moment_two):
    local_grad = grads[0, 0]
    group_sum = lax.psum_scatter(
        local_grad.astype(jnp.float32).astype(jnp.bfloat16),
        "shard",
        scatter_dimension=0,
        tiled=True,
    ).astype(jnp.float32)
    total = lax.psum(group_sum, "replica")
    updated, first, second = adam_update(total, master, moment_one, moment_two)
    weights = lax.all_gather(updated.astype(jnp.bfloat16), "shard", axis=0, tiled=True)
    return (updated, first, second, weights)


def solution(mesh):
    placed = (
        P("replica", "shard", None, None),
        P("shard", None),
        P("shard", None),
        P("shard", None),
    )
    return jax.shard_map(
        local,
        mesh=mesh,
        in_specs=placed,
        out_specs=(P("shard", None), P("shard", None), P("shard", None), P()),
        check_vma=False,
    )
```

profile of v0, /device:TPU:7, one launch (start us, length us, event | category | flops | bytes accessed | tf_op | source)
XLA Modules:
  0.0 392.6 jit_solution(3998188347045665005)
XLA Ops:
  7.2 0.0 copy-start.2
  7.2 0.0 copy-start.1
  7.2 0.0 copy-start
  7.2 0.0 reduce-scatter.2.cloned.1.call-start
  7.2 0.7 reduce-scatter.2.cloned.1.call-update
  7.9 0.0 all-gather.2.cloned.1.call-start
  8.0 216.9 %reduce-scatter.2.cloned.1.call-done = bf16[16,8192]{1,0:T(8,128)(2,1)} async-done(((bf16[256,8192]{1,0:T(8,128)(2,1)}), bf16[16,8192]{1,0:T(8,128)(2,1)}) %reduce-scatter.2.cloned.1.call-update) | async-done | bytes 262160 | tf_op jit(solution)/shard_map/reduce_scatter | solution.py:20
  224.9 59.7 %all-reduce.1 = f32[16,8192]{1,0:T(8,128)S(1)} all-reduce(bf16[16,8192]{1,0:T(8,128)(2,1)} %reduce-scatter.2.cloned.1.call-done), channel_id=1, replica_groups=mesh['replica'=16,'shard'=16] {'replica'}, use_global_device_ids=true, to_apply=%region_1.0 | all-reduce | flops 131072 | bytes 786432 | tf_op jit(solution)/shard_map/psum | solution.py:26
  284.6 0.0 copy-done.2
  284.6 0.0 copy-done.1
  284.6 0.0 copy-done
  284.6 1.5 fusion.1
  286.1 0.0 all-gather.2.cloned.1.call-update
  286.1 95.0 %all-gather.2.cloned.1.call-done = bf16[256,8192]{1,0:T(8,128)(2,1)} async-done(((bf16[16,8192]{1,0:T(8,128)(2,1)}), bf16[256,8192]{1,0:T(8,128)(2,1)}) %all-gather.2.cloned.1.call-update) | async-done | bytes 4194320 | tf_op jit(solution)/shard_map/all_gather | solution.py:28
  381.1 4.6 %copy.11 = bf16[256,8192]{1,0:T(8,128)(2,1)} copy(bf16[256,8192]{1,0:T(8,128)(2,1)} %all-gather.2.cloned.1.call-done) | data formatting | bytes 8388608
Async XLA Ops:
  7.2 277.4 %copy-start.2 = (f32[16,8192]{1,0:T(8,128)S(1)}, f32[16,8192]{1,0:T(8,128)}, u32[]{:S(2)}) copy-start(f32[16,8192]{1,0:T(8,128)} %param.7) | copy-start | bytes 1572868
  7.2 277.4 %copy-start.1 = (f32[16,8192]{1,0:T(8,128)S(1)}, f32[16,8192]{1,0:T(8,128)}, u32[]{:S(2)}) copy-start(f32[16,8192]{1,0:T(8,128)} %param.6) | copy-start | bytes 1572868
  7.2 277.4 %copy-start = (f32[16,8192]{1,0:T(8,128)S(1)}, f32[16,8192]{1,0:T(8,128)}, u32[]{:S(2)}) copy-start(f32[16,8192]{1,0:T(8,128)} %param.5) | copy-start | bytes 1572868
  7.2 217.7 %reduce-scatter.2.cloned.1.call-start = ((), (), s32[]{:S(2)}) async-start(), calls=%async_computation.1 | async-start | bytes 4456448 | tf_op jit(solution)/shard_map/reduce_scatter | solution.py:20
  7.9 373.2 %all-gather.2.cloned.1.call-start = ((), (), s32[]{:S(2)}) async-start(), calls=%async_computation.2 | async-start | bytes 4456448 | tf_op jit(solution)/shard_map/all_gather | solution.py:28
Sparse Core Ops, SparseCore 0:
  12.0 212.8 reduce-scatter.1
  286.3 94.8 all-gather.1
where the time goes:
time: 397 us; the launch traced here: 393 us
  waiting for transfers between devices  313 us (79%)
  blocking collectives  59.7 us (15%)
  between operations  14.1 us (4%)
  local copies, waits for them, and re-layouts  4.65 us (1%)
    reduce_scatter x1, waiting for transfers between devices, local(): lax.psum_scatter(local_grad.astype(jnp.float32).astype(jnp.bfloat16), 'sh...  217 us
    all_gather x1, waiting for transfers between devices, local(): lax.all_gather(updated.astype(jnp.bfloat16), 'shard', axis=0, tiled=True)  95 us
    psum x1, blocking collectives, local(): total = lax.psum(group_sum, 'replica')  59.7 us
  transfers between devices with their start and end apart: 2, of which 2 were waited for; matrix products, arithmetic and copies ran while one was open for 0% of the time, Pallas kernels for 0%

commit v1 on v0

--- a/solution.py
+++ b/solution.py
@@ -4,6 +4,10 @@
 from jax.sharding import PartitionSpec as P
 
 STEP = 20
+AXES = ("replica", "shard")
+BF = jnp.bfloat16
+F32 = jnp.float32
+U32 = jnp.uint32
 
 
 def adam_update(total, master, moment_one, moment_two):
@@ -15,17 +19,131 @@
     return (updated, first, second)
 
 
+def flat(x, y, z, c):
+    return ((y % 2) * 8 + x * 2 + c) * 16 + (y // 2) * 8 + z
+
+
+def pairs(move):
+    return [
+        (flat(x, y, z, c), flat(*move(x, y, z, c)))
+        for x in range(4)
+        for y in range(4)
+        for z in range(8)
+        for c in range(2)
+    ]
+
+
+def send(value, move):
+    return lax.ppermute(value, AXES, pairs(move))
+
+
+def core(value):
+    return send(value, lambda x, y, z, c: (x, y, z, 1 - c))
+
+
+def along_x(value, k):
+    return send(value, lambda x, y, z, c: ((x + k) % 4, y, z, c))
+
+
+def along_y(value, k):
+    return send(value, lambda x, y, z, c: (x, (y + k) % 4, z, c))
+
+
+def cut(value, row, col, rows, cols):
+    row, col = jnp.asarray(row, U32), jnp.asarray(col, U32)
+    return lax.dynamic_slice(value, (row, col), (rows, cols))
+
+
+def put(whole, value, row, col):
+    row, col = jnp.asarray(row, U32), jnp.asarray(col, U32)
+    return lax.dynamic_update_slice(whole, value, (row, col))
+
+
+def add(values):
+    total = values[0].astype(F32)
+    for value in values[1:]:
+        total = total + value.astype(F32)
+    return total
+
+
 def local(grads, master, moment_one, moment_two):
-    local_grad = grads[0, 0]
-    group_sum = lax.psum_scatter(
-        local_grad.astype(jnp.float32).astype(jnp.bfloat16),
-        "shard",
-        scatter_dimension=0,
-        tiled=True,
-    ).astype(jnp.float32)
-    total = lax.psum(group_sum, "replica")
+    g = grads[0, 0]
+    r = lax.axis_index("replica").astype(U32)
+    s = lax.axis_index("shard").astype(U32)
+    yl, x, c = r >> 3, (r >> 1) & 3, r & 1
+    yh = s >> 3
+    y = yh * 2 + yl
+    half, far = c * 4096, (1 - c) * 4096
+    z_groups = [list(range(8)), list(range(8, 16))]
+
+    def a_at(t):
+        return U32(0), t * 512
+
+    def b_at(t):
+        return (t >> 1) * 128, 2048 + (t & 1) * 1024
+
+    mine_a, mine_b = {}, {}
+    for k in (2, 1, 3, 0):
+        row, col = a_at((x + k) & 3)
+        got = core(cut(g, row, far + col, 256, 512))
+        mine_a[k] = add([cut(g, row, half + col, 256, 512), got]).astype(BF)
+        row, col = b_at((y + k) & 3)
+        got = core(cut(g, row, far + col, 128, 1024))
+        mine_b[k] = add([cut(g, row, half + col, 128, 1024), got]).astype(BF)
+    got_a = {k: along_x(mine_a[k], k) for k in (2, 1, 3)}
+    got_b = {k: along_y(mine_b[k], k) for k in (2, 1, 3)}
+    a = add([mine_a[0], got_a[1], got_a[3], got_a[2]]).astype(BF)
+    b = add([mine_b[0], got_b[1], got_b[3], got_b[2]]).astype(BF)
+
+    def a2(t):
+        return cut(a, (t >> 1) * 128, (t & 1) * 256, 128, 256)
+
+    def b2(t):
+        return cut(b, 0, t * 256, 128, 256)
+
+    got_a = {k: along_y(a2((y + k) & 3), k) for k in (2, 1, 3)}
+    got_b = {k: along_x(b2((x + k) & 3), k) for k in (2, 1, 3)}
+    a = add([a2(y), got_a[1], got_a[3], got_a[2]]).astype(BF)
+    b = add([b2(x), got_b[1], got_b[3], got_b[2]]).astype(BF)
+    ab = jnp.concatenate([a, b], axis=1).reshape(8, 16, 512)
+    ab = lax.all_to_all(ab, "shard", 0, 0, tiled=True, axis_index_groups=z_groups)
+    piece = add([ab[i] for i in range(8)]).astype(BF)
+
+    a_col = half + x * 512 + yl * 256
+    b_col = half + 2048 + yl * 1024 + x * 256
+
+    def own(v):
+        return jnp.concatenate([cut(v, 0, a_col, 16, 256), cut(v, 0, b_col, 16, 256)], axis=1)
+
+    w = adam_update(piece.astype(F32), own(master), own(moment_one), own(moment_two))[0].astype(BF)
+    w = lax.all_to_all(
+        jnp.broadcast_to(w[None], (8, 16, 512)), "shard", 0, 0, tiled=True, axis_index_groups=z_groups
+    ).reshape(128, 512)
+    a, b = w[:, :256], w[:, 256:]
+    wa = jnp.zeros((256, 512), BF)
+    wb = jnp.zeros((128, 1024), BF)
+    for k in (0, 1, 3, 2):
+        t = (y + 4 - k) & 3
+        wa = put(wa, along_y(a, k) if k else a, (t >> 1) * 128, (t & 1) * 256)
+        t = (x + 4 - k) & 3
+        wb = put(wb, along_x(b, k) if k else b, 0, t * 256)
+    weights = jnp.zeros((256, 8192), BF)
+    for k in (0, 1, 3, 2):
+        piece_a = along_x(wa, k) if k else wa
+        row, col = a_at((x + 4 - k) & 3)
+        weights = put(weights, piece_a, row, half + col)
+        weights = put(weights, core(piece_a), row, far + col)
+        piece_b = along_y(wb, k) if k else wb
+        row, col = b_at((y + 4 - k) & 3)
+        weights = put(weights, piece_b, row, half + col)
+        weights = put(weights, core(piece_b), row, far + col)
+
+    rows = lax.all_to_all(jnp.broadcast_to(piece[None], (16, 16, 512)), "replica", 0, 0, tiled=True)
+    rows = rows.reshape(2, 4, 2, 16, 2, 256)
+    rows_a = rows[:, :, :, :, 0].transpose(3, 2, 1, 0, 4).reshape(16, 2, 2048)
+    rows_b = rows[:, :, :, :, 1].transpose(3, 2, 0, 1, 4).reshape(16, 2, 2048)
+    total = jnp.concatenate([rows_a, rows_b], axis=2).reshape(16, 8192).astype(F32)
     updated, first, second = adam_update(total, master, moment_one, moment_two)
-    weights = lax.all_gather(updated.astype(jnp.bfloat16), "shard", axis=0, tiled=True)
     return (updated, first, second, weights)
 
 

time: 397 us -> 146 us (0.37)
  waiting for transfers between devices: 313 us -> 24.1 us
  starting transfers between devices: 0.08 us -> 62 us
  blocking collectives: 59.7 us -> 10.3 us
  local copies, waits for them, and re-layouts: 4.65 us -> 40.4 us
  between operations: 14.1 us -> 1.2 us
  other arithmetic: 1.47 us -> 7.25 us
    reduce_scatter x1 -> x0, waiting for transfers between devices: 217 us -> none  [local(): lax.psum_scatter(local_grad.astype(jnp.float32).astype(jnp.bfloat16), 'sh...]
    all_gather x1 -> x0, waiting for transfers between devices: 95 us -> none  [local(): lax.all_gather(updated.astype(jnp.bfloat16), 'shard', axis=0, tiled=True)]
    psum x1 -> x0, blocking collectives: 59.7 us -> none  [local(): total = lax.psum(group_sum, 'replica')]
    ppermute x0 -> x40, starting transfers between devices: none -> 39 us  [send(): return lax.ppermute(value, AXES, pairs(move))]
    dynamic_update_slice x0 -> x22, local copies, waits for them, and re-layouts: none -> 31.8 us  [put(): return lax.dynamic_update_slice(whole, value, (row, col))]
    all_to_all x0 -> x2, starting transfers between devices: none -> 23 us  [the longest x1 14.8 us: local(): lax.all_to_all(jnp.broadcast_to(piece[None], (16, 16, 512)), 'replica', 0...]
    ppermute x0 -> x40, waiting for transfers between devices: none -> 16.2 us  [send(): return lax.ppermute(value, AXES, pairs(move))]
    all_to_all x0 -> x1, blocking collectives: none -> 10.3 us  [local(): lax.all_to_all(jnp.broadcast_to(w[None], (8, 16, 512)), 'shard', 0, 0, ti...]
  transfers between devices with their start and end apart: 2 -> 42, of which waited for: 2 -> 8; matrix products, arithmetic and copies ran while one was open for 0% -> 27% of each run, Pallas kernels for 0% -> 0%
where the time goes in v1:
time: 146 us; the launch traced here: 145 us
  starting transfers between devices  62 us (42%)
  local copies, waits for them, and re-layouts  40.4 us (28%)
  waiting for transfers between devices  24.1 us (17%)
  blocking collectives  10.3 us (7%)
  other arithmetic  7.25 us (5%)
    ppermute x40, starting transfers between devices, send(): return lax.ppermute(value, AXES, pairs(move))  39 us
    dynamic_update_slice x22, local copies, waits for them, and re-layouts, put(): return lax.dynamic_update_slice(whole, value, (row, col))  31.8 us
    ppermute x40, waiting for transfers between devices, send(): return lax.ppermute(value, AXES, pairs(move))  16.2 us
    all_to_all x1, starting transfers between devices, local(): lax.all_to_all(jnp.broadcast_to(piece[None], (16, 16, 512)), 'replica', 0...  14.8 us
    all_to_all x1, blocking collectives, local(): lax.all_to_all(jnp.broadcast_to(w[None], (8, 16, 512)), 'shard', 0, 0, ti...  10.3 us
    all_to_all x1, starting transfers between devices, local(): lax.all_to_all(ab, 'shard', 0, 0, tiled=True, axis_index_groups=z_groups)  8.19 us
    all_to_all x1, waiting for transfers between devices, local(): lax.all_to_all(ab, 'shard', 0, 0, tiled=True, axis_index_groups=z_groups)  7.86 us
    dynamic_slice x4, local copies, waits for them, and re-layouts, cut(): return lax.dynamic_slice(value, (row, col), (rows, cols))  4.12 us
  transfers between devices with their start and end apart: 42, of which 8 were waited for; matrix products, arithmetic and copies ran while one was open for 27% of the time, Pallas kernels for 0%

profile of v1, /device:TPU:7, one launch (start us, length us, event | category | flops | bytes accessed | tf_op | source)
XLA Modules:
  0.0 145.2 jit_solution(14368942831630261543)
XLA Ops:
  0.7 2.0 %dynamic-slice_bitcast_fusion.3 = (bf16[128,1024]{1,0:T(8,128)(2,1)}, bf16[128,1024]{1,0:T(8,128)(2,1)S(1)}, bf16[128,1024]{1,0:T(8,128)(2,1)S(1)}, bf16[128,1024]{1,0:T(8,128)(2,1)S(1)}) fusion(bf16[1,1,256,8192]{3,2,1,0:T(8,128)(2,1)} %param.4, u32[]{:T(128)S(6)} %mul.227, u32[]{:T(128)S(6)} %add.326, u32[]{:T(128)S(6)} %mul.223, u32[]{:T(128)S(6)} %add.335, ...), kind=kLoop, calls=%fused_computation.26 | loop fusion | bytes 2097184 | tf_op jit(solution)/shard_map/dynamic_slice | solution.py:54
  2.7 0.7 collective-permute-start.11
  3.4 0.5 collective-permute-start.15
  3.9 2.0 %dynamic-slice_bitcast_fusion.7 = (bf16[256,512]{1,0:T(8,128)(2,1)S(1)}, bf16[256,512]{1,0:T(8,128)(2,1)S(1)}, bf16[256,512]{1,0:T(8,128)(2,1)}, bf16[256,512]{1,0:T(8,128)(2,1)}) fusion(bf16[1,1,256,8192]{3,2,1,0:T(8,128)(2,1)} %param.4, u32[]{:T(128)S(6)} %add.300, u32[]{:T(128)S(6)} %add.314, u32[]{:T(128)S(6)} %add.309, u32[]{:T(128)S(6)} %add.304), kind=kLoop, calls=%fused_computation.30 | loop fusion | bytes 2097168 | tf_op jit(solution)/shard_map/dynamic_slice | solution.py:54
  5.9 0.5 collective-permute-start.3
  6.4 0.5 collective-permute-start
  7.0 1.4 fusion.3
  8.5 1.4 collective-permute-start.12
  9.9 1.5 %collective-permute-start.14 = (bf16[128,1024]{1,0:T(8,128)(2,1)S(1)}, bf16[128,1024]{1,0:T(8,128)(2,1)S(1)}, u32[]{:S(2)}, u32[]{:S(2)}) collective-permute-start(bf16[128,1024]{1,0:T(8,128)(2,1)S(1)} %get-tuple-element.21), channel_id=1, source_target_pairs={{0,136},{16,152},{1,137},{17,153},{2,138},{18,154},{3,139},{19,155... | collective-permute-start | bytes 786440 | tf_op jit(solution)/shard_map/ppermute | solution.py:37
  11.4 1.5 %collective-permute-start.16 = (bf16[128,1024]{1,0:T(8,128)(2,1)S(1)}, bf16[128,1024]{1,0:T(8,128)(2,1)S(1)}, u32[]{:S(2)}, u32[]{:S(2)}) collective-permute-start(bf16[128,1024]{1,0:T(8,128)(2,1)S(1)} %get-tuple-element.22), channel_id=1, source_target_pairs={{0,8},{16,24},{1,9},{17,25},{2,10},{18,26},{3,11},{19,27},{4,12},{... | collective-permute-start | bytes 786440 | tf_op jit(solution)/shard_map/ppermute | solution.py:37
  13.0 1.3 fusion.7
  14.6 2.8 %collective-permute-done.12 = bf16[128,1024]{1,0:T(8,128)(2,1)S(1)} collective-permute-done((bf16[128,1024]{1,0:T(8,128)(2,1)S(1)}, bf16[128,1024]{1,0:T(8,128)(2,1)S(1)}, u32[]{:S(2)}, u32[]{:S(2)}) %collective-permute-start.12) | collective-permute-done | bytes 262176 | tf_op jit(solution)/shard_map/ppermute | solution.py:37
  17.4 0.5 collective-permute-start.4
  17.9 2.9 %collective-permute-start.6 = (bf16[256,512]{1,0:T(8,128)(2,1)S(1)}, bf16[256,512]{1,0:T(8,128)(2,1)S(1)}, u32[]{:S(2)}, u32[]{:S(2)}) collective-permute-start(bf16[256,512]{1,0:T(8,128)(2,1)S(1)} %get-tuple-element.14), channel_id=1, source_target_pairs={{0,64},{16,80},{1,65},{17,81},{2,66},{18,82},{3,67},{19,83},{4,68}... | collective-permute-start | bytes 786440 | tf_op jit(solution)/shard_map/ppermute | solution.py:37
  20.8 3.3 %collective-permute-done.16 = bf16[128,1024]{1,0:T(8,128)(2,1)S(1)} collective-permute-done((bf16[128,1024]{1,0:T(8,128)(2,1)S(1)}, bf16[128,1024]{1,0:T(8,128)(2,1)S(1)}, u32[]{:S(2)}, u32[]{:S(2)}) %collective-permute-start.16) | collective-permute-done | bytes 262176 | tf_op jit(solution)/shard_map/ppermute | solution.py:37
  24.1 1.2 add_convert_fusion
  25.6 1.2 collective-permute-start.18
  26.8 1.1 collective-permute-start.19
  28.0 1.1 add_convert_fusion.1
  29.1 2.1 %collective-permute-start.7 = (bf16[128,256]{1,0:T(8,128)(2,1)S(1)}, bf16[128,256]{1,0:T(8,128)(2,1)S(1)}, u32[]{:S(2)}, u32[]{:S(2)}) collective-permute-start(bf16[128,256]{1,0:T(8,128)(2,1)S(1)} %get-tuple-element.31), channel_id=1, source_target_pairs={{0,128},{16,144},{1,129},{17,145},{2,130},{18,146},{3,131},{19,147... | collective-permute-start | bytes 196616 | tf_op jit(solution)/shard_map/ppermute | solution.py:37
  31.3 1.2 collective-permute-start.8
  32.4 1.1 collective-permute-start.9
  33.6 0.7 collective-permute-done.7
  34.3 0.4 collective-permute-done.8
  34.7 2.7 %collective-permute-done.9 = bf16[128,256]{1,0:T(8,128)(2,1)S(1)} collective-permute-done((bf16[128,256]{1,0:T(8,128)(2,1)S(1)}, bf16[128,256]{1,0:T(8,128)(2,1)S(1)}, u32[]{:S(2)}, u32[]{:S(2)}) %collective-permute-start.9) | collective-permute-done | bytes 65568 | tf_op jit(solution)/shard_map/ppermute | solution.py:37
  37.4 0.7 pad_maximum_fusion
  38.0 8.2 %all-to-all-start = ((bf16[8,16,512]{2,1,0:T(8,128)(2,1)}), bf16[8,16,512]{2,1,0:T(8,128)(2,1)S(1)}, u32[]{:S(2)}, u32[]{:S(2)}) async-start(bf16[8,16,512]{2,1,0:T(8,128)(2,1)} %bitcast.16), calls=%async_computation | async-start | bytes 262144 | tf_op jit(solution)/shard_map/all_to_all | solution.py:109
  46.3 7.9 %all-to-all-done = bf16[8,16,512]{2,1,0:T(8,128)(2,1)S(1)} async-done(((bf16[8,16,512]{2,1,0:T(8,128)(2,1)}), bf16[8,16,512]{2,1,0:T(8,128)(2,1)S(1)}, u32[]{:S(2)}, u32[]{:S(2)}) %all-to-all-start) | async-done | bytes 131104 | tf_op jit(solution)/shard_map/all_to_all | solution.py:109
  54.2 10.3 %all_to_all.15 = bf16[8,16,512]{2,1,0:T(8,128)(2,1)S(1)} all-to-all(bf16[8,16,512]{2,1,0:T(8,128)(2,1)S(1)} %broadcast_in_dim.30), channel_id=1, replica_groups={{0,1,2,3,4,5,6,7},{8,9,10,11,12,13,14,15},{16,17,18,19,20,21,22,23},{24..., dimensions={0} | all-to-all | bytes 262144 | tf_op jit(solution)/shard_map/all_to_all | solution.py:119
  64.5 0.7 broadcast_in_dim.26
  65.3 14.8 %all-to-all-start.1 = ((bf16[16,16,512]{2,1,0:T(8,128)(2,1)}), bf16[16,16,512]{2,1,0:T(8,128)(2,1)S(1)}, u32[]{:S(2)}, u32[]{:S(2)}) async-start(bf16[16,16,512]{2,1,0:T(8,128)(2,1)} %broadcast_in_dim.26), calls=%async_computation.1 | async-start | bytes 524288 | tf_op jit(solution)/shard_map/all_to_all | solution.py:141
  80.4 1.4 collective-permute-start.25
  81.7 1.2 collective-permute-start.20
  82.9 2.0 %collective-permute-start.21 = (bf16[128,256]{1,0:T(8,128)(2,1)S(1)}, bf16[128,256]{1,0:T(8,128)(2,1)S(1)}, u32[]{:S(2)}, u32[]{:S(2)}) collective-permute-start(bf16[128,256]{1,0:T(8,128)(2,1)S(1)} %get-tuple-element.40), channel_id=1, source_target_pairs={{0,136},{16,152},{1,137},{17,153},{2,138},{18,154},{3,139},{19,155... | collective-permute-start | bytes 196616 | tf_op jit(solution)/shard_map/ppermute | solution.py:37
  84.9 1.5 %collective-permute-start.22 = (bf16[128,256]{1,0:T(8,128)(2,1)S(1)}, bf16[128,256]{1,0:T(8,128)(2,1)S(1)}, u32[]{:S(2)}, u32[]{:S(2)}) collective-permute-start(bf16[128,256]{1,0:T(8,128)(2,1)S(1)} %get-tuple-element.40), channel_id=1, source_target_pairs={{0,8},{16,24},{1,9},{17,25},{2,10},{18,26},{3,11},{19,27},{4,12},{... | collective-permute-start | bytes 196616 | tf_op jit(solution)/shard_map/ppermute | solution.py:37
  86.4 0.6 fusion.22
  87.6 1.3 collective-permute-start.26
  88.8 0.8 dynamic_update_slice.73
  89.7 1.2 dynamic_update_slice.74
  90.8 1.2 dynamic_update_slice.75
  92.0 2.2 %collective-permute-start.23 = (bf16[256,512]{1,0:T(8,128)(2,1)S(1)}, bf16[256,512]{1,0:T(8,128)(2,1)S(1)}, u32[]{:S(2)}, u32[]{:S(2)}) collective-permute-start(bf16[256,512]{1,0:T(8,128)(2,1)S(1)} %dynamic_update_slice.75), channel_id=1, source_target_pairs={{0,16},{16,0},{1,17},{17,1},{2,18},{18,2},{3,19},{19,3},{4,20},{20... | collective-permute-start | bytes 786440 | tf_op jit(solution)/shard_map/ppermute | solution.py:37
  94.2 1.8 %collective-permute-start.28 = (bf16[256,512]{1,0:T(8,128)(2,1)S(1)}, bf16[256,512]{1,0:T(8,128)(2,1)S(1)}, u32[]{:S(2)}, u32[]{:S(2)}) collective-permute-start(bf16[256,512]{1,0:T(8,128)(2,1)S(1)} %dynamic_update_slice.75), channel_id=1, source_target_pairs={{0,32},{16,48},{1,33},{17,49},{2,34},{18,50},{3,35},{19,51},{4,36}... | collective-permute-start | bytes 786440 | tf_op jit(solution)/shard_map/ppermute | solution.py:37
  96.0 0.5 collective-permute-start.27
  96.5 1.1 collective-permute-start.30
  97.6 1.6 %collective-permute-start.34 = (bf16[128,1024]{1,0:T(8,128)(2,1)S(1)}, bf16[128,1024]{1,0:T(8,128)(2,1)S(1)}, u32[]{:S(2)}, u32[]{:S(2)}) collective-permute-start(bf16[128,1024]{1,0:T(8,128)(2,1)S(1)} %constant_dynamic-update-slice_fusion.6), channel_id=1, source_target_pairs={{0,136},{16,152},{1,137},{17,153},{2,138},{18,154},{3,139},{19,155... | collective-permute-start | bytes 786440 | tf_op jit(solution)/shard_map/ppermute | solution.py:37
  99.2 1.4 multiply_subtract_fusion
  100.6 1.5 %collective-permute-start.36 = (bf16[256,512]{1,0:T(8,128)(2,1)S(1)}, bf16[256,512]{1,0:T(8,128)(2,1)S(1)}, u32[]{:S(2)}, u32[]{:S(2)}) collective-permute-start(bf16[256,512]{1,0:T(8,128)(2,1)S(1)} %dynamic_update_slice.75), channel_id=1, source_target_pairs={{0,64},{16,80},{1,65},{17,81},{2,66},{18,82},{3,67},{19,83},{4,68}... | collective-permute-start | bytes 786440 | tf_op jit(solution)/shard_map/ppermute | solution.py:37
  102.1 2.1 %collective-permute-start.38 = (bf16[128,1024]{1,0:T(8,128)(2,1)S(1)}, bf16[128,1024]{1,0:T(8,128)(2,1)S(1)}, u32[]{:S(2)}, u32[]{:S(2)}) collective-permute-start(bf16[128,1024]{1,0:T(8,128)(2,1)S(1)} %constant_dynamic-update-slice_fusion.6), channel_id=1, source_target_pairs={{0,8},{16,24},{1,9},{17,25},{2,10},{18,26},{3,11},{19,27},{4,12},{... | collective-permute-start | bytes 786440 | tf_op jit(solution)/shard_map/ppermute | solution.py:37
  104.1 1.3 collective-permute-done.30
  105.4 1.0 collective-permute-start.29
  106.4 0.5 broadcast_in_dim.27
  106.9 4.9 %collective-permute-done.32 = bf16[256,512]{1,0:T(8,128)(2,1)S(1)} collective-permute-done((bf16[256,512]{1,0:T(8,128)(2,1)S(1)}, bf16[256,512]{1,0:T(8,128)(2,1)S(1)}, u32[]{:S(2)}, u32[]{:S(2)}) %collective-permute-start.32) | collective-permute-done | bytes 262176 | tf_op jit(solution)/shard_map/ppermute | solution.py:37
  111.9 1.3 collective-permute-start.31
  113.2 4.3 %dynamic_update_slice.82 = bf16[256,8192]{1,0:T(8,128)(2,1)S(1)} dynamic-update-slice(bf16[256,8192]{1,0:T(8,128)(2,1)S(1)} %constant_dynamic-update-slice_fusion.10, bf16[128,1024]{1,0:T(8,128)(2,1)S(1)} %constant_dynamic-update-slice_fusion.6, u32[]{:T(128)S(6)} %mul.259, u32[]{:T(128)S(6)} %add.373) | dynamic-update-slice | bytes 524292 | tf_op jit(solution)/shard_map/dynamic_update_slice | solution.py:59
  117.5 4.3 %dynamic_update_slice.83 = bf16[256,8192]{1,0:T(8,128)(2,1)S(1)} dynamic-update-slice(bf16[256,8192]{1,0:T(8,128)(2,1)S(1)} %dynamic_update_slice.82, bf16[128,1024]{1,0:T(8,128)(2,1)S(1)} %collective-permute-done.27, u32[]{:T(128)S(6)} %mul.259, u32[]{:T(128)S(6)} %add.374) | dynamic-update-slice | bytes 524292 | tf_op jit(solution)/shard_map/dynamic_update_slice | solution.py:59
  122.0 0.6 collective-permute-start.35
  122.7 0.4 collective-permute-start.39
  123.1 2.5 %dynamic_update_slice.86 = bf16[256,8192]{1,0:T(8,128)(2,1)S(1)} dynamic-update-slice(bf16[256,8192]{1,0:T(8,128)(2,1)S(1)} %constant_dynamic-update-slice_fusion.4, bf16[128,1024]{1,0:T(8,128)(2,1)S(1)} %collective-permute-done.30, u32[]{:T(128)S(6)} %mul.223, u32[]{:T(128)S(6)} %add.334) | dynamic-update-slice | bytes 524292 | tf_op jit(solution)/shard_map/dynamic_update_slice | solution.py:59
  125.6 3.4 %dynamic_update_slice.87 = bf16[256,8192]{1,0:T(8,128)(2,1)S(1)} dynamic-update-slice(bf16[256,8192]{1,0:T(8,128)(2,1)S(1)} %dynamic_update_slice.86, bf16[128,1024]{1,0:T(8,128)(2,1)S(1)} %collective-permute-done.31, u32[]{:T(128)S(6)} %mul.223, u32[]{:T(128)S(6)} %add.335) | dynamic-update-slice | bytes 524292 | tf_op jit(solution)/shard_map/dynamic_update_slice | solution.py:59
  129.0 2.9 %dynamic_update_slice.90 = bf16[256,8192]{1,0:T(8,128)(2,1)S(1)} dynamic-update-slice(bf16[256,8192]{1,0:T(8,128)(2,1)S(1)} %constant_dynamic-update-slice_fusion.2, bf16[128,1024]{1,0:T(8,128)(2,1)S(1)} %collective-permute-done.34, u32[]{:T(128)S(6)} %mul.221, u32[]{:T(128)S(6)} %add.329) | dynamic-update-slice | bytes 524292 | tf_op jit(solution)/shard_map/dynamic_update_slice | solution.py:59
  132.0 4.3 %dynamic_update_slice.91 = bf16[256,8192]{1,0:T(8,128)(2,1)S(1)} dynamic-update-slice(bf16[256,8192]{1,0:T(8,128)(2,1)S(1)} %dynamic_update_slice.90, bf16[128,1024]{1,0:T(8,128)(2,1)S(1)} %collective-permute-done.35, u32[]{:T(128)S(6)} %mul.221, u32[]{:T(128)S(6)} %add.330) | dynamic-update-slice | bytes 524292 | tf_op jit(solution)/shard_map/dynamic_update_slice | solution.py:59
  136.4 3.4 %dynamic_update_slice.94 = bf16[256,8192]{1,0:T(8,128)(2,1)S(1)} dynamic-update-slice(bf16[256,8192]{1,0:T(8,128)(2,1)S(1)} %constant_dynamic-update-slice_fusion, bf16[128,1024]{1,0:T(8,128)(2,1)S(1)} %collective-permute-done.38, u32[]{:T(128)S(6)} %mul.225, u32[]{:T(128)S(6)} %add.339) | dynamic-update-slice | bytes 524292 | tf_op jit(solution)/shard_map/dynamic_update_slice | solution.py:59
  139.8 3.4 %dynamic_update_slice.95 = bf16[256,8192]{1,0:T(8,128)(2,1)S(1)} dynamic-update-slice(bf16[256,8192]{1,0:T(8,128)(2,1)S(1)} %dynamic_update_slice.94, bf16[128,1024]{1,0:T(8,128)(2,1)S(1)} %collective-permute-done.39, u32[]{:T(128)S(6)} %mul.225, u32[]{:T(128)S(6)} %add.340) | dynamic-update-slice | bytes 524292 | tf_op jit(solution)/shard_map/dynamic_update_slice | solution.py:59
  143.2 2.0 %copy-done = bf16[256,8192]{1,0:T(8,128)(2,1)} copy-done((bf16[256,8192]{1,0:T(8,128)(2,1)}, bf16[256,8192]{1,0:T(8,128)(2,1)S(1)}, u32[]{:S(2)}) %copy-start) | copy-done | bytes 4194328
  (82 shorter events, 2.3 us)
Async XLA Ops:
  2.7 3.8 %collective-permute-start.11 = (bf16[128,1024]{1,0:T(8,128)(2,1)S(1)}, bf16[128,1024]{1,0:T(8,128)(2,1)S(1)}, u32[]{:S(2)}, u32[]{:S(2)}) collective-permute-start(bf16[128,1024]{1,0:T(8,128)(2,1)S(1)} %get-tuple-element.18), channel_id=1, source_target_pairs={{0,16},{16,0},{1,17},{17,1},{2,18},{18,2},{3,19},{19,3},{4,20},{20... | collective-permute-start | bytes 786440 | tf_op jit(solution)/shard_map/ppermute | solution.py:37
  3.4 3.1 %collective-permute-start.13 = (bf16[128,1024]{1,0:T(8,128)(2,1)S(1)}, bf16[128,1024]{1,0:T(8,128)(2,1)S(1)}, u32[]{:S(2)}, u32[]{:S(2)}) collective-permute-start(bf16[128,1024]{1,0:T(8,128)(2,1)S(1)} %get-tuple-element.17), channel_id=1, source_target_pairs={{0,16},{16,0},{1,17},{17,1},{2,18},{18,2},{3,19},{19,3},{4,20},{20... | collective-permute-start | bytes 786440 | tf_op jit(solution)/shard_map/ppermute | solution.py:37
  3.4 3.6 %collective-permute-start.15 = (bf16[128,1024]{1,0:T(8,128)(2,1)S(1)}, bf16[128,1024]{1,0:T(8,128)(2,1)S(1)}, u32[]{:S(2)}, u32[]{:S(2)}) collective-permute-start(bf16[128,1024]{1,0:T(8,128)(2,1)S(1)} %get-tuple-element.19), channel_id=1, source_target_pairs={{0,16},{16,0},{1,17},{17,1},{2,18},{18,2},{3,19},{19,3},{4,20},{20... | collective-permute-start | bytes 786440 | tf_op jit(solution)/shard_map/ppermute | solution.py:37
  5.9 2.6 %collective-permute-start.1 = (bf16[256,512]{1,0:T(8,128)(2,1)}, bf16[256,512]{1,0:T(8,128)(2,1)S(1)}, u32[]{:S(2)}, u32[]{:S(2)}) collective-permute-start(bf16[256,512]{1,0:T(8,128)(2,1)} %get-tuple-element.12), channel_id=1, source_target_pairs={{0,16},{16,0},{1,17},{17,1},{2,18},{18,2},{3,19},{19,3},{4,20},{20... | collective-permute-start | bytes 786440 | tf_op jit(solution)/shard_map/ppermute | solution.py:37
  5.9 4.0 %collective-permute-start.3 = (bf16[256,512]{1,0:T(8,128)(2,1)}, bf16[256,512]{1,0:T(8,128)(2,1)S(1)}, u32[]{:S(2)}, u32[]{:S(2)}) collective-permute-start(bf16[256,512]{1,0:T(8,128)(2,1)} %get-tuple-element.11), channel_id=1, source_target_pairs={{0,16},{16,0},{1,17},{17,1},{2,18},{18,2},{3,19},{19,3},{4,20},{20... | collective-permute-start | bytes 786440 | tf_op jit(solution)/shard_map/ppermute | solution.py:37
  6.4 5.0 %collective-permute-start.5 = (bf16[256,512]{1,0:T(8,128)(2,1)S(1)}, bf16[256,512]{1,0:T(8,128)(2,1)S(1)}, u32[]{:S(2)}, u32[]{:S(2)}) collective-permute-start(bf16[256,512]{1,0:T(8,128)(2,1)S(1)} %get-tuple-element.10), channel_id=1, source_target_pairs={{0,16},{16,0},{1,17},{17,1},{2,18},{18,2},{3,19},{19,3},{4,20},{20... | collective-permute-start | bytes 786440 | tf_op jit(solution)/shard_map/ppermute | solution.py:37
  6.4 19.2 %collective-permute-start = (bf16[256,512]{1,0:T(8,128)(2,1)S(1)}, bf16[256,512]{1,0:T(8,128)(2,1)S(1)}, u32[]{:S(2)}, u32[]{:S(2)}) collective-permute-start(bf16[256,512]{1,0:T(8,128)(2,1)S(1)} %get-tuple-element.9), channel_id=1, source_target_pairs={{0,16},{16,0},{1,17},{17,1},{2,18},{18,2},{3,19},{19,3},{4,20},{20... | collective-permute-start | bytes 786440 | tf_op jit(solution)/shard_map/ppermute | solution.py:37
  6.9 7.3 %collective-permute-start.10 = (bf16[128,1024]{1,0:T(8,128)(2,1)}, bf16[128,1024]{1,0:T(8,128)(2,1)S(1)}, u32[]{:S(2)}, u32[]{:S(2)}) collective-permute-start(bf16[128,1024]{1,0:T(8,128)(2,1)} %get-tuple-element.16), channel_id=1, source_target_pairs={{0,16},{16,0},{1,17},{17,1},{2,18},{18,2},{3,19},{19,3},{4,20},{20... | collective-permute-start | bytes 786440 | tf_op jit(solution)/shard_map/ppermute | solution.py:37
  8.4 37.8 %copy-start.1 = (f32[16,8192]{1,0:T(8,128)S(1)}, f32[16,8192]{1,0:T(8,128)}, u32[]{:S(2)}) copy-start(f32[16,8192]{1,0:T(8,128)} %param.5) | copy-start | bytes 1572868
  8.5 37.8 %copy-start.2 = (f32[16,8192]{1,0:T(8,128)S(1)}, f32[16,8192]{1,0:T(8,128)}, u32[]{:S(2)}) copy-start(f32[16,8192]{1,0:T(8,128)} %param.7) | copy-start | bytes 1572868
  8.5 37.8 %copy-start.3 = (f32[16,8192]{1,0:T(8,128)S(1)}, f32[16,8192]{1,0:T(8,128)}, u32[]{:S(2)}) copy-start(f32[16,8192]{1,0:T(8,128)} %param.6) | copy-start | bytes 1572868
  8.5 8.9 %collective-permute-start.12 = (bf16[128,1024]{1,0:T(8,128)(2,1)S(1)}, bf16[128,1024]{1,0:T(8,128)(2,1)S(1)}, u32[]{:S(2)}, u32[]{:S(2)}) collective-permute-start(bf16[128,1024]{1,0:T(8,128)(2,1)S(1)} %get-tuple-element.20), channel_id=1, source_target_pairs={{0,128},{16,144},{1,129},{17,145},{2,130},{18,146},{3,131},{19,147... | collective-permute-start | bytes 786440 | tf_op jit(solution)/shard_map/ppermute | solution.py:37
  9.9 8.0 %collective-permute-start.14 = (bf16[128,1024]{1,0:T(8,128)(2,1)S(1)}, bf16[128,1024]{1,0:T(8,128)(2,1)S(1)}, u32[]{:S(2)}, u32[]{:S(2)}) collective-permute-start(bf16[128,1024]{1,0:T(8,128)(2,1)S(1)} %get-tuple-element.21), channel_id=1, source_target_pairs={{0,136},{16,152},{1,137},{17,153},{2,138},{18,154},{3,139},{19,155... | collective-permute-start | bytes 786440 | tf_op jit(solution)/shard_map/ppermute | solution.py:37
  11.4 12.7 %collective-permute-start.16 = (bf16[128,1024]{1,0:T(8,128)(2,1)S(1)}, bf16[128,1024]{1,0:T(8,128)(2,1)S(1)}, u32[]{:S(2)}, u32[]{:S(2)}) collective-permute-start(bf16[128,1024]{1,0:T(8,128)(2,1)S(1)} %get-tuple-element.22), channel_id=1, source_target_pairs={{0,8},{16,24},{1,9},{17,25},{2,10},{18,26},{3,11},{19,27},{4,12},{... | collective-permute-start | bytes 786440 | tf_op jit(solution)/shard_map/ppermute | solution.py:37
  14.3 12.6 %collective-permute-start.2 = (bf16[256,512]{1,0:T(8,128)(2,1)S(1)}, bf16[256,512]{1,0:T(8,128)(2,1)S(1)}, u32[]{:S(2)}, u32[]{:S(2)}) collective-permute-start(bf16[256,512]{1,0:T(8,128)(2,1)S(1)} %get-tuple-element.13), channel_id=1, source_target_pairs={{0,32},{16,48},{1,33},{17,49},{2,34},{18,50},{3,35},{19,51},{4,36}... | collective-permute-start | bytes 786440 | tf_op jit(solution)/shard_map/ppermute | solution.py:37
  17.4 10.6 %collective-permute-start.4 = (bf16[256,512]{1,0:T(8,128)(2,1)S(1)}, bf16[256,512]{1,0:T(8,128)(2,1)S(1)}, u32[]{:S(2)}, u32[]{:S(2)}) collective-permute-start(bf16[256,512]{1,0:T(8,128)(2,1)S(1)} %get-tuple-element.15), channel_id=1, source_target_pairs={{0,96},{16,112},{1,97},{17,113},{2,98},{18,114},{3,99},{19,115},{4... | collective-permute-start | bytes 786440 | tf_op jit(solution)/shard_map/ppermute | solution.py:37
  17.9 10.1 %collective-permute-start.6 = (bf16[256,512]{1,0:T(8,128)(2,1)S(1)}, bf16[256,512]{1,0:T(8,128)(2,1)S(1)}, u32[]{:S(2)}, u32[]{:S(2)}) collective-permute-start(bf16[256,512]{1,0:T(8,128)(2,1)S(1)} %get-tuple-element.14), channel_id=1, source_target_pairs={{0,64},{16,80},{1,65},{17,81},{2,66},{18,82},{3,67},{19,83},{4,68}... | collective-permute-start | bytes 786440 | tf_op jit(solution)/shard_map/ppermute | solution.py:37
  25.3 7.1 %collective-permute-start.17 = (bf16[128,256]{1,0:T(8,128)(2,1)S(1)}, bf16[128,256]{1,0:T(8,128)(2,1)S(1)}, u32[]{:S(2)}, u32[]{:S(2)}) collective-permute-start(bf16[128,256]{1,0:T(8,128)(2,1)S(1)} %get-tuple-element.34), channel_id=1, source_target_pairs={{0,32},{16,48},{1,33},{17,49},{2,34},{18,50},{3,35},{19,51},{4,36}... | collective-permute-start | bytes 196616 | tf_op jit(solution)/shard_map/ppermute | solution.py:37
  25.6 7.9 %collective-permute-start.18 = (bf16[128,256]{1,0:T(8,128)(2,1)S(1)}, bf16[128,256]{1,0:T(8,128)(2,1)S(1)}, u32[]{:S(2)}, u32[]{:S(2)}) collective-permute-start(bf16[128,256]{1,0:T(8,128)(2,1)S(1)} %get-tuple-element.36), channel_id=1, source_target_pairs={{0,96},{16,112},{1,97},{17,113},{2,98},{18,114},{3,99},{19,115},{4... | collective-permute-start | bytes 196616 | tf_op jit(solution)/shard_map/ppermute | solution.py:37
  26.8 6.7 %collective-permute-start.19 = (bf16[128,256]{1,0:T(8,128)(2,1)S(1)}, bf16[128,256]{1,0:T(8,128)(2,1)S(1)}, u32[]{:S(2)}, u32[]{:S(2)}) collective-permute-start(bf16[128,256]{1,0:T(8,128)(2,1)S(1)} %get-tuple-element.35), channel_id=1, source_target_pairs={{0,64},{16,80},{1,65},{17,81},{2,66},{18,82},{3,67},{19,83},{4,68}... | collective-permute-start | bytes 196616 | tf_op jit(solution)/shard_map/ppermute | solution.py:37
  29.1 5.1 %collective-permute-start.7 = (bf16[128,256]{1,0:T(8,128)(2,1)S(1)}, bf16[128,256]{1,0:T(8,128)(2,1)S(1)}, u32[]{:S(2)}, u32[]{:S(2)}) collective-permute-start(bf16[128,256]{1,0:T(8,128)(2,1)S(1)} %get-tuple-element.31), channel_id=1, source_target_pairs={{0,128},{16,144},{1,129},{17,145},{2,130},{18,146},{3,131},{19,147... | collective-permute-start | bytes 196616 | tf_op jit(solution)/shard_map/ppermute | solution.py:37
  31.3 3.4 %collective-permute-start.8 = (bf16[128,256]{1,0:T(8,128)(2,1)S(1)}, bf16[128,256]{1,0:T(8,128)(2,1)S(1)}, u32[]{:S(2)}, u32[]{:S(2)}) collective-permute-start(bf16[128,256]{1,0:T(8,128)(2,1)S(1)} %get-tuple-element.33), channel_id=1, source_target_pairs={{0,136},{16,152},{1,137},{17,153},{2,138},{18,154},{3,139},{19,155... | collective-permute-start | bytes 196616 | tf_op jit(solution)/shard_map/ppermute | solution.py:37
  32.4 4.9 %collective-permute-start.9 = (bf16[128,256]{1,0:T(8,128)(2,1)S(1)}, bf16[128,256]{1,0:T(8,128)(2,1)S(1)}, u32[]{:S(2)}, u32[]{:S(2)}) collective-permute-start(bf16[128,256]{1,0:T(8,128)(2,1)S(1)} %get-tuple-element.32), channel_id=1, source_target_pairs={{0,8},{16,24},{1,9},{17,25},{2,10},{18,26},{3,11},{19,27},{4,12},{... | collective-permute-start | bytes 196616 | tf_op jit(solution)/shard_map/ppermute | solution.py:37
  38.0 16.1 %all-to-all-start = ((bf16[8,16,512]{2,1,0:T(8,128)(2,1)}), bf16[8,16,512]{2,1,0:T(8,128)(2,1)S(1)}, u32[]{:S(2)}, u32[]{:S(2)}) async-start(bf16[8,16,512]{2,1,0:T(8,128)(2,1)} %bitcast.16), calls=%async_computation | async-start | bytes 262144 | tf_op jit(solution)/shard_map/all_to_all | solution.py:109
  65.3 21.1 %all-to-all-start.1 = ((bf16[16,16,512]{2,1,0:T(8,128)(2,1)}), bf16[16,16,512]{2,1,0:T(8,128)(2,1)S(1)}, u32[]{:S(2)}, u32[]{:S(2)}) async-start(bf16[16,16,512]{2,1,0:T(8,128)(2,1)} %broadcast_in_dim.26), calls=%async_computation.1 | async-start | bytes 524288 | tf_op jit(solution)/shard_map/all_to_all | solution.py:141
  80.2 15.8 %collective-permute-start.24 = (bf16[128,256]{1,0:T(8,128)(2,1)S(1)}, bf16[128,256]{1,0:T(8,128)(2,1)S(1)}, u32[]{:S(2)}, u32[]{:S(2)}) collective-permute-start(bf16[128,256]{1,0:T(8,128)(2,1)S(1)} %get-tuple-element.37), channel_id=1, source_target_pairs={{0,32},{16,48},{1,33},{17,49},{2,34},{18,50},{3,35},{19,51},{4,36}... | collective-permute-start | bytes 196616 | tf_op jit(solution)/shard_map/ppermute | solution.py:37
  80.4 15.6 %collective-permute-start.25 = (bf16[128,256]{1,0:T(8,128)(2,1)S(1)}, bf16[128,256]{1,0:T(8,128)(2,1)S(1)}, u32[]{:S(2)}, u32[]{:S(2)}) collective-permute-start(bf16[128,256]{1,0:T(8,128)(2,1)S(1)} %get-tuple-element.37), channel_id=1, source_target_pairs={{0,96},{16,112},{1,97},{17,113},{2,98},{18,114},{3,99},{19,115},{4... | collective-permute-start | bytes 196616 | tf_op jit(solution)/shard_map/ppermute | solution.py:37
  81.7 5.8 %collective-permute-start.20 = (bf16[128,256]{1,0:T(8,128)(2,1)S(1)}, bf16[128,256]{1,0:T(8,128)(2,1)S(1)}, u32[]{:S(2)}, u32[]{:S(2)}) collective-permute-start(bf16[128,256]{1,0:T(8,128)(2,1)S(1)} %get-tuple-element.40), channel_id=1, source_target_pairs={{0,128},{16,144},{1,129},{17,145},{2,130},{18,146},{3,131},{19,147... | collective-permute-start | bytes 196616 | tf_op jit(solution)/shard_map/ppermute | solution.py:37
  82.9 6.7 %collective-permute-start.21 = (bf16[128,256]{1,0:T(8,128)(2,1)S(1)}, bf16[128,256]{1,0:T(8,128)(2,1)S(1)}, u32[]{:S(2)}, u32[]{:S(2)}) collective-permute-start(bf16[128,256]{1,0:T(8,128)(2,1)S(1)} %get-tuple-element.40), channel_id=1, source_target_pairs={{0,136},{16,152},{1,137},{17,153},{2,138},{18,154},{3,139},{19,155... | collective-permute-start | bytes 196616 | tf_op jit(solution)/shard_map/ppermute | solution.py:37
  84.9 5.9 %collective-permute-start.22 = (bf16[128,256]{1,0:T(8,128)(2,1)S(1)}, bf16[128,256]{1,0:T(8,128)(2,1)S(1)}, u32[]{:S(2)}, u32[]{:S(2)}) collective-permute-start(bf16[128,256]{1,0:T(8,128)(2,1)S(1)} %get-tuple-element.40), channel_id=1, source_target_pairs={{0,8},{16,24},{1,9},{17,25},{2,10},{18,26},{3,11},{19,27},{4,12},{... | collective-permute-start | bytes 196616 | tf_op jit(solution)/shard_map/ppermute | solution.py:37
  87.6 8.4 %collective-permute-start.26 = (bf16[128,256]{1,0:T(8,128)(2,1)S(1)}, bf16[128,256]{1,0:T(8,128)(2,1)S(1)}, u32[]{:S(2)}, u32[]{:S(2)}) collective-permute-start(bf16[128,256]{1,0:T(8,128)(2,1)S(1)} %get-tuple-element.37), channel_id=1, source_target_pairs={{0,64},{16,80},{1,65},{17,81},{2,66},{18,82},{3,67},{19,83},{4,68}... | collective-permute-start | bytes 196616 | tf_op jit(solution)/shard_map/ppermute | solution.py:37
  92.0 5.6 %collective-permute-start.23 = (bf16[256,512]{1,0:T(8,128)(2,1)S(1)}, bf16[256,512]{1,0:T(8,128)(2,1)S(1)}, u32[]{:S(2)}, u32[]{:S(2)}) collective-permute-start(bf16[256,512]{1,0:T(8,128)(2,1)S(1)} %dynamic_update_slice.75), channel_id=1, source_target_pairs={{0,16},{16,0},{1,17},{17,1},{2,18},{18,2},{3,19},{19,3},{4,20},{20... | collective-permute-start | bytes 786440 | tf_op jit(solution)/shard_map/ppermute | solution.py:37
  94.2 7.9 %collective-permute-start.28 = (bf16[256,512]{1,0:T(8,128)(2,1)S(1)}, bf16[256,512]{1,0:T(8,128)(2,1)S(1)}, u32[]{:S(2)}, u32[]{:S(2)}) collective-permute-start(bf16[256,512]{1,0:T(8,128)(2,1)S(1)} %dynamic_update_slice.75), channel_id=1, source_target_pairs={{0,32},{16,48},{1,33},{17,49},{2,34},{18,50},{3,35},{19,51},{4,36}... | collective-permute-start | bytes 786440 | tf_op jit(solution)/shard_map/ppermute | solution.py:37
  96.0 4.6 %collective-permute-start.27 = (bf16[128,1024]{1,0:T(8,128)(2,1)S(1)}, bf16[128,1024]{1,0:T(8,128)(2,1)S(1)}, u32[]{:S(2)}, u32[]{:S(2)}) collective-permute-start(bf16[128,1024]{1,0:T(8,128)(2,1)S(1)} %constant_dynamic-update-slice_fusion.6), channel_id=1, source_target_pairs={{0,16},{16,0},{1,17},{17,1},{2,18},{18,2},{3,19},{19,3},{4,20},{20... | collective-permute-start | bytes 786440 | tf_op jit(solution)/shard_map/ppermute | solution.py:37
  96.5 8.9 %collective-permute-start.30 = (bf16[128,1024]{1,0:T(8,128)(2,1)S(1)}, bf16[128,1024]{1,0:T(8,128)(2,1)S(1)}, u32[]{:S(2)}, u32[]{:S(2)}) collective-permute-start(bf16[128,1024]{1,0:T(8,128)(2,1)S(1)} %constant_dynamic-update-slice_fusion.6), channel_id=1, source_target_pairs={{0,128},{16,144},{1,129},{17,145},{2,130},{18,146},{3,131},{19,147... | collective-permute-start | bytes 786440 | tf_op jit(solution)/shard_map/ppermute | solution.py:37
  97.6 14.3 %collective-permute-start.32 = (bf16[256,512]{1,0:T(8,128)(2,1)S(1)}, bf16[256,512]{1,0:T(8,128)(2,1)S(1)}, u32[]{:S(2)}, u32[]{:S(2)}) collective-permute-start(bf16[256,512]{1,0:T(8,128)(2,1)S(1)} %dynamic_update_slice.75), channel_id=1, source_target_pairs={{0,96},{16,112},{1,97},{17,113},{2,98},{18,114},{3,99},{19,115},{4... | collective-permute-start | bytes 786440 | tf_op jit(solution)/shard_map/ppermute | solution.py:37
  97.6 24.2 %collective-permute-start.34 = (bf16[128,1024]{1,0:T(8,128)(2,1)S(1)}, bf16[128,1024]{1,0:T(8,128)(2,1)S(1)}, u32[]{:S(2)}, u32[]{:S(2)}) collective-permute-start(bf16[128,1024]{1,0:T(8,128)(2,1)S(1)} %constant_dynamic-update-slice_fusion.6), channel_id=1, source_target_pairs={{0,136},{16,152},{1,137},{17,153},{2,138},{18,154},{3,139},{19,155... | collective-permute-start | bytes 786440 | tf_op jit(solution)/shard_map/ppermute | solution.py:37
  100.6 21.4 %collective-permute-start.36 = (bf16[256,512]{1,0:T(8,128)(2,1)S(1)}, bf16[256,512]{1,0:T(8,128)(2,1)S(1)}, u32[]{:S(2)}, u32[]{:S(2)}) collective-permute-start(bf16[256,512]{1,0:T(8,128)(2,1)S(1)} %dynamic_update_slice.75), channel_id=1, source_target_pairs={{0,64},{16,80},{1,65},{17,81},{2,66},{18,82},{3,67},{19,83},{4,68}... | collective-permute-start | bytes 786440 | tf_op jit(solution)/shard_map/ppermute | solution.py:37
  102.1 20.5 %collective-permute-start.38 = (bf16[128,1024]{1,0:T(8,128)(2,1)S(1)}, bf16[128,1024]{1,0:T(8,128)(2,1)S(1)}, u32[]{:S(2)}, u32[]{:S(2)}) collective-permute-start(bf16[128,1024]{1,0:T(8,128)(2,1)S(1)} %constant_dynamic-update-slice_fusion.6), channel_id=1, source_target_pairs={{0,8},{16,24},{1,9},{17,25},{2,10},{18,26},{3,11},{19,27},{4,12},{... | collective-permute-start | bytes 786440 | tf_op jit(solution)/shard_map/ppermute | solution.py:37
  105.4 17.2 %collective-permute-start.29 = (bf16[256,512]{1,0:T(8,128)(2,1)S(1)}, bf16[256,512]{1,0:T(8,128)(2,1)S(1)}, u32[]{:S(2)}, u32[]{:S(2)}) collective-permute-start(bf16[256,512]{1,0:T(8,128)(2,1)S(1)} %collective-permute-done.28), channel_id=1, source_target_pairs={{0,16},{16,0},{1,17},{17,1},{2,18},{18,2},{3,19},{19,3},{4,20},{20... | collective-permute-start | bytes 786440 | tf_op jit(solution)/shard_map/ppermute | solution.py:37
  111.9 13.7 %collective-permute-start.31 = (bf16[128,1024]{1,0:T(8,128)(2,1)S(1)}, bf16[128,1024]{1,0:T(8,128)(2,1)S(1)}, u32[]{:S(2)}, u32[]{:S(2)}) collective-permute-start(bf16[128,1024]{1,0:T(8,128)(2,1)S(1)} %collective-permute-done.30), channel_id=1, source_target_pairs={{0,16},{16,0},{1,17},{17,1},{2,18},{18,2},{3,19},{19,3},{4,20},{20... | collective-permute-start | bytes 786440 | tf_op jit(solution)/shard_map/ppermute | solution.py:37
  121.8 7.2 %collective-permute-start.33 = (bf16[256,512]{1,0:T(8,128)(2,1)S(1)}, bf16[256,512]{1,0:T(8,128)(2,1)S(1)}, u32[]{:S(2)}, u32[]{:S(2)}) collective-permute-start(bf16[256,512]{1,0:T(8,128)(2,1)S(1)} %collective-permute-done.32), channel_id=1, source_target_pairs={{0,16},{16,0},{1,17},{17,1},{2,18},{18,2},{3,19},{19,3},{4,20},{20... | collective-permute-start | bytes 786440 | tf_op jit(solution)/shard_map/ppermute | solution.py:37
  122.0 10.0 %collective-permute-start.35 = (bf16[128,1024]{1,0:T(8,128)(2,1)S(1)}, bf16[128,1024]{1,0:T(8,128)(2,1)S(1)}, u32[]{:S(2)}, u32[]{:S(2)}) collective-permute-start(bf16[128,1024]{1,0:T(8,128)(2,1)S(1)} %collective-permute-done.34), channel_id=1, source_target_pairs={{0,16},{16,0},{1,17},{17,1},{2,18},{18,2},{3,19},{19,3},{4,20},{20... | collective-permute-start | bytes 786440 | tf_op jit(solution)/shard_map/ppermute | solution.py:37
  122.5 13.8 %collective-permute-start.37 = (bf16[256,512]{1,0:T(8,128)(2,1)S(1)}, bf16[256,512]{1,0:T(8,128)(2,1)S(1)}, u32[]{:S(2)}, u32[]{:S(2)}) collective-permute-start(bf16[256,512]{1,0:T(8,128)(2,1)S(1)} %collective-permute-done.36), channel_id=1, source_target_pairs={{0,16},{16,0},{1,17},{17,1},{2,18},{18,2},{3,19},{19,3},{4,20},{20... | collective-permute-start | bytes 786440 | tf_op jit(solution)/shard_map/ppermute | solution.py:37
  122.7 17.1 %collective-permute-start.39 = (bf16[128,1024]{1,0:T(8,128)(2,1)S(1)}, bf16[128,1024]{1,0:T(8,128)(2,1)S(1)}, u32[]{:S(2)}, u32[]{:S(2)}) collective-permute-start(bf16[128,1024]{1,0:T(8,128)(2,1)S(1)} %collective-permute-done.38), channel_id=1, source_target_pairs={{0,16},{16,0},{1,17},{17,1},{2,18},{18,2},{3,19},{19,3},{4,20},{20... | collective-permute-start | bytes 786440 | tf_op jit(solution)/shard_map/ppermute | solution.py:37
  143.2 2.0 %copy-start = (bf16[256,8192]{1,0:T(8,128)(2,1)}, bf16[256,8192]{1,0:T(8,128)(2,1)S(1)}, u32[]{:S(2)}) copy-start(bf16[256,8192]{1,0:T(8,128)(2,1)S(1)} %dynamic_update_slice.95) | copy-start | bytes 12582916

commit v2 on v0

v2 whole, which is shorter than its diff:
```python
import jax
import jax.numpy as jnp
from jax import lax
from jax.experimental import pallas as pl
from jax.sharding import PartitionSpec as P


STEP = 20
AXES = ("replica", "shard")
BF = jnp.bfloat16
F32 = jnp.float32
U32 = jnp.uint32


def adam_update(total, master, moment_one, moment_two):
    first = 0.9 * moment_one + 0.1 * total
    second = 0.95 * moment_two + 0.05 * total * total
    first_hat = first / (1.0 - 0.9**STEP)
    second_hat = second / (1.0 - 0.95**STEP)
    updated = master - 0.0003 * (first_hat / (jnp.sqrt(second_hat) + 1e-08) + 0.1 * master)
    return (updated, first, second)


def flat(x, y, z, c):
    return ((y % 2) * 8 + x * 2 + c) * 16 + (y // 2) * 8 + z


def send(value, move):
    pairs = [
        (flat(x, y, z, c), flat(*move(x, y, z, c)))
        for x in range(4)
        for y in range(4)
        for z in range(8)
        for c in range(2)
    ]
    return lax.ppermute(value, AXES, pairs)


def over_core(value):
    return send(value, lambda x, y, z, c: (x, y, z, 1 - c))


def along_a(value, k):
    return send(value, lambda x, y, z, c: ((x + k) % 4, y, z, c) if c == 0 else (x, (y + k) % 4, z, c))


def along_b(value, k):
    return send(value, lambda x, y, z, c: (x, (y + k) % 4, z, c) if c == 0 else ((x + k) % 4, y, z, c))


def tiles(value):
    rows, cols = value.shape
    return value.reshape(rows // 8, 8, cols // 128, 128).transpose(0, 2, 1, 3)


def untiles(value):
    rt, ct = value.shape[:2]
    return value.transpose(0, 2, 1, 3).reshape(rt * 8, ct * 128)


def cut(value, starts, sizes):
    starts = [jnp.asarray(i, U32) for i in starts] + [U32(0)] * (value.ndim - len(starts))
    return lax.dynamic_slice(value, starts, tuple(sizes) + value.shape[len(sizes) :])


def put(whole, value, starts):
    starts = [jnp.asarray(i, U32) for i in starts] + [U32(0)] * (whole.ndim - len(starts))
    return lax.dynamic_update_slice(whole, value, starts)


def unset(shape, dtype):
    return pl.pallas_call(
        lambda out: None, out_shape=jax.ShapeDtypeStruct(shape, dtype), out_specs=pl.BlockSpec(memory_space=pl.ANY)
    )()


def add(values):
    total = values[0].astype(F32)
    for value in values[1:]:
        total = total + value.astype(F32)
    return total.astype(BF)


def local(grads, master, moment_one, moment_two):
    g = tiles(grads[0, 0])
    r = lax.axis_index("replica").astype(U32)
    s = lax.axis_index("shard").astype(U32)
    yl, x, c = r >> 3, (r >> 1) & 3, r & 1
    yh = s >> 3
    y = yh * 2 + yl
    core1 = c == 1
    a_pos, a_far = jnp.where(core1, y, x), jnp.where(core1, x, y)
    b_pos = jnp.where(core1, x, y)
    z_groups = [list(range(8)), list(range(8, 16))]

    def block(core_is_1, base, t, j):
        row = jnp.where(core_is_1, t >> 1, U32(j)) * 16
        col = jnp.where(core_is_1, 2 * (t & 1) + j, t) * 8
        return row, base + col

    half, far = c * 32, (1 - c) * 32
    states = [tiles(v) for v in (master, moment_one, moment_two)]
    col = half + jnp.where(core1, yl * 16 + x * 4, x * 8 + yl * 4)
    own_states = [cut(v, (0, col), (2, 4)) for v in states]

    def quarter(value, core_is_1, base, t):
        halves = cut(value, ((t >> 1) * 16, base + (t & 1) * 16), (16, 16)).reshape(256, 8, 128)
        columns = cut(value, (0, base + t * 8), (32, 8)).reshape(256, 8, 128)
        return jnp.where(core_is_1, halves, columns)

    def outgoing(source, k):
        return quarter(source, c == 0, far, (a_far + k) & 3)

    def merged(own, got, k):
        return add([quarter(own, core1, U32(0), (a_pos + k) & 3), got])

    out, g = lax.optimization_barrier((outgoing(g, 2), g))
    sent = {2: over_core(out)}
    own, g = lax.optimization_barrier((cut(g, (0, half), (32, 32)), g))
    mine = {2: merged(own, sent[2], 2)}
    mine[2], g, own = lax.optimization_barrier((mine[2], g, own))
    out = {k: outgoing(g, k) for k in (1, 3, 0)}
    for k in (1, 3, 0):
        sent[k] = over_core(out[k])
    for k in (1, 3, 0):
        mine[k], own = lax.optimization_barrier((merged(own, sent[k], k), own))
    got = {k: along_a(mine[k], k) for k in (2, 1, 3)}
    sums = add([mine[0], got[1], got[3], got[2]])

    def part(t):
        rows = cut(sums.reshape(32, 8, 8, 128), ((t >> 1) * 16, (t & 1) * 4), (16, 4))
        return jnp.where(core1, cut(sums.reshape(16, 16, 8, 128), (0, t * 4), (16, 4)), rows)

    got = {k: along_b(part((b_pos + k) & 3), k) for k in (2, 1, 3)}
    sums = add([part(b_pos), got[1], got[3], got[2]])
    sums, own_states = lax.optimization_barrier((sums, own_states))
    sums = lax.all_to_all(sums.reshape(8, 2, 4, 8, 128), "shard", 0, 0, tiled=True, axis_index_groups=z_groups)
    piece = add([sums[i] for i in range(8)])

    w = adam_update(piece.astype(F32), *own_states)[0].astype(BF)
    other = over_core(piece)
    w = lax.all_to_all(
        jnp.broadcast_to(w[None], (8, 2, 4, 8, 128)), "shard", 0, 0, tiled=True, axis_index_groups=z_groups
    ).reshape(16, 4, 8, 128)
    whole = unset((2, 16, 8, 8, 128), BF)
    for k in (0, 1, 3, 2):
        t = (b_pos + 4 - k) & 3
        whole = put(whole, (along_b(w, k) if k else w)[None], (t >> 1, 0, (t & 1) * 4))
    got = {k: along_a(whole, k) for k in (2, 1, 3)}
    got[0] = whole
    weights = unset((32, 64, 8, 128), BF)
    for k in (0, 1, 3, 2):
        for j in (0, 1):
            weights = put(weights, got[k][j], block(core1, half, (a_pos + 4 - k) & 3, j))
        theirs = over_core(got[k])
        for j in (0, 1):
            weights = put(weights, theirs[j], block(c == 0, far, (a_far + 4 - k) & 3, j))

    rows = jnp.stack([jnp.where(core1, other, piece), jnp.where(core1, piece, other)])
    other = send(rows, lambda x, y, z, c: (x, y ^ 1, z, c))
    rows = jnp.stack([jnp.where(yl == 1, other, rows), jnp.where(yl == 1, rows, other)])
    moved = {k: send(rows, lambda x, y, z, c, k=k: ((x + k) % 4, y, z, c)) for k in (2, 1, 3)}
    moved[0] = rows
    total = unset((4, 2, 2, 2, 4, 8, 128), BF)
    for k in (0, 1, 3, 2):
        total = put(total, moved[k][None], ((x + 4 - k) & 3,))
    total0 = total[:, :, 0].transpose(2, 0, 1, 3, 4, 5).reshape(2, 32, 8, 128)
    total1 = total[:, :, 1].transpose(2, 1, 0, 3, 4, 5).reshape(2, 32, 8, 128)
    total = jnp.concatenate([total0, total1], axis=1).astype(F32)
    out = adam_update(total, *states)
    return (*[untiles(v) for v in out], untiles(weights))


def solution(mesh):
    placed = (
        P("replica", "shard", None, None),
        P("shard", None),
        P("shard", None),
        P("shard", None),
    )
    return jax.shard_map(
        local,
        mesh=mesh,
        in_specs=placed,
        out_specs=(P("shard", None), P("shard", None), P("shard", None), P()),
        check_vma=False,
    )
```

time: 397 us -> 103 us (0.26)
  waiting for transfers between devices: 313 us -> 34.4 us
  blocking collectives: 59.7 us -> 14.8 us
  starting transfers between devices: 0.08 us -> 33 us
  between operations: 14.1 us -> 1.32 us
  local copies, waits for them, and re-layouts: 4.65 us -> 12.7 us
  other arithmetic: 1.47 us -> 6.25 us
    reduce_scatter x1 -> x0, waiting for transfers between devices: 217 us -> none  [local(): lax.psum_scatter(local_grad.astype(jnp.float32).astype(jnp.bfloat16), 'sh...]
    all_gather x1 -> x0, waiting for transfers between devices: 95 us -> none  [local(): lax.all_gather(updated.astype(jnp.bfloat16), 'shard', axis=0, tiled=True)]
    psum x1 -> x0, blocking collectives: 59.7 us -> none  [local(): total = lax.psum(group_sum, 'replica')]
    ppermute x0 -> x25, waiting for transfers between devices: none -> 33.9 us  [send(): return lax.ppermute(value, AXES, pairs)]
    ppermute x0 -> x25, starting transfers between devices: none -> 29.7 us  [send(): return lax.ppermute(value, AXES, pairs)]
    all_to_all x0 -> x1, blocking collectives: none -> 14.8 us  [local(): lax.all_to_all(sums.reshape(8, 2, 4, 8, 128), 'shard', 0, 0, tiled=True,...]
  transfers between devices with their start and end apart: 2 -> 26, of which waited for: 2 -> 13; matrix products, arithmetic and copies ran while one was open for 0% -> 10% of each run, Pallas kernels for 0% -> 0%
where the time goes in v2:
time: 103 us
  waiting for transfers between devices  34.4 us (33%)
  starting transfers between devices  33 us (32%)
  blocking collectives  14.8 us (14%)
  local copies, waits for them, and re-layouts  12.7 us (12%)
  other arithmetic  6.25 us (6%)
  between operations  1.32 us (1%)
    ppermute x25, waiting for transfers between devices, send(): return lax.ppermute(value, AXES, pairs)  33.9 us
    ppermute x25, starting transfers between devices, send(): return lax.ppermute(value, AXES, pairs)  29.7 us
    all_to_all x1, blocking collectives, local(): lax.all_to_all(sums.reshape(8, 2, 4, 8, 128), 'shard', 0, 0, tiled=True,...  14.8 us
    all_to_all x1, starting transfers between devices, local(): lax.all_to_all(jnp.broadcast_to(w[None], (8, 2, 4, 8, 128)), 'shard', 0,...  3.37 us
    dynamic_slice x13, local copies, waits for them, and re-layouts, cut(): lax.dynamic_slice(value, starts, tuple(sizes) + value.shape[len(sizes):])  3.16 us
    unnamed x14, local copies, waits for them, and re-layouts  2.86 us
    convert_element_type x6, other arithmetic, add(): return total.astype(BF)  2.61 us
    dynamic_update_slice x23, local copies, waits for them, and re-layouts, put(): return lax.dynamic_update_slice(whole, value, starts)  2.6 us
  transfers between devices with their start and end apart: 26, of which 13 were waited for; matrix products, arithmetic and copies ran while one was open for 10% of the time, Pallas kernels for 0%

profile of v2, /device:TPU:7, one launch (start us, length us, event | category | flops | bytes accessed | tf_op | source)
XLA Modules:
  0.0 102.5 jit_solution(4307835207628736037)
XLA Ops:
  0.7 1.1 %constant_dynamic-slice_fusion.15 = bf16[32,8,8,128]{3,1,2,0:T(8,128)(2,1)S(1)} fusion(bf16[32,8,64,128]{3,1,2,0:T(8,128)(2,1)} %bitcast.205, u32[]{:T(128)S(6)} %add.275), kind=kLoop, calls=%fused_computation.110 | loop fusion | bytes 1048580 | tf_op jit(solution)/shard_map/dynamic-slice.1
  1.7 1.1 %constant_dynamic-slice_fusion.16 = bf16[16,8,16,128]{3,1,2,0:T(8,128)(2,1)S(1)} fusion(bf16[32,8,64,128]{3,1,2,0:T(8,128)(2,1)} %bitcast.206, u32[]{:T(128)S(6)} %mul.333, u32[]{:T(128)S(6)} %add.274), kind=kLoop, calls=%fused_computation.111 | loop fusion | bytes 1048584 | tf_op jit(solution)/shard_map/dynamic-slice
  2.9 0.9 bitcast_select_fusion
  3.8 0.7 collective-permute-start
  4.4 1.7 %constant_dynamic-slice_fusion.14 = bf16[32,32,8,128]{3,2,1,0:T(8,128)(2,1)S(1)} fusion(bf16[32,64,8,128]{3,2,1,0:T(8,128)(2,1)} %bitcast.207, u32[]{:T(128)S(6)} %mul.337), kind=kLoop, calls=%fused_computation.109 | loop fusion | bytes 4194308 | tf_op jit(solution)/shard_map/dynamic_slice | solution.py:63
  6.2 0.0 copy-start
  6.4 1.4 %add_convert_fusion.4 = bf16[256,8,128]{2,1,0:T(8,128)(2,1)S(1)} fusion(bf16[256,8,128]{2,1,0:T(8,128)(2,1)} %collective-permute-done, bf16[32,8,8,128]{3,2,1,0:T(8,128)(2,1)S(1)} %constant_dynamic-slice_fusion.12, bf16[16,16,8,128]{3,2,1,0:T(8,128)(2,1)S(1)} %constant_dynamic-slice_fusion.13, pred[]{:T(512)S(6)} %eq.7), kind=kLoop, calls=%fused_computation.4 | loop fusion | flops 1310720 | bytes 2097153 | tf_op jit(solution)/shard_map/convert_element_type | solution.py:81
  7.8 0.8 copy-done
  8.6 0.1 constant_dynamic-slice_fusion
  8.7 0.2 constant_dynamic-slice_fusion.1
  8.9 0.1 bitcast_select_fusion.5
  9.1 0.1 collective-permute-start.1
  9.2 0.1 bitcast_select_fusion.1
  9.3 0.6 collective-permute-start.3
  9.9 0.1 bitcast_select_fusion.3
  10.0 0.1 collective-permute-start.2
  10.1 3.0 %collective-permute-start.6 = (bf16[256,8,128]{2,1,0:T(8,128)(2,1)S(1)}, bf16[256,8,128]{2,1,0:T(8,128)(2,1)S(1)}, u32[]{:S(2)}, u32[]{:S(2)}) collective-permute-start(bf16[256,8,128]{2,1,0:T(8,128)(2,1)S(1)} %add_convert_fusion.4), channel_id=1, source_target_pairs={{0,64},{16,24},{1,65},{17,25},{2,66},{18,26},{3,67},{19,27},{4,68}... | collective-permute-start | bytes 1572872 | tf_op jit(solution)/shard_map/ppermute | solution.py:36
  13.2 0.3 add_convert_fusion.3
  13.6 0.3 add_convert_fusion.2
  13.9 0.0 copy-start.4
  13.9 1.8 %collective-permute-start.5 = (bf16[256,8,128]{2,1,0:T(8,128)(2,1)S(1)}, bf16[256,8,128]{2,1,0:T(8,128)(2,1)S(1)}, u32[]{:S(2)}, u32[]{:S(2)}) collective-permute-start(bf16[256,8,128]{2,1,0:T(8,128)(2,1)S(1)} %add_convert_fusion.2), channel_id=1, source_target_pairs={{0,96},{16,152},{1,97},{17,153},{2,98},{18,154},{3,99},{19,155},{4... | collective-permute-start | bytes 1572872 | tf_op jit(solution)/shard_map/ppermute | solution.py:36
  15.8 0.3 add_convert_fusion.1
  16.1 3.9 %collective-permute-done.6 = bf16[256,8,128]{2,1,0:T(8,128)(2,1)S(1)} collective-permute-done((bf16[256,8,128]{2,1,0:T(8,128)(2,1)S(1)}, bf16[256,8,128]{2,1,0:T(8,128)(2,1)S(1)}, u32[]{:S(2)}, u32[]{:S(2)}) %collective-permute-start.6) | collective-permute-done | bytes 524320 | tf_op jit(solution)/shard_map/ppermute | solution.py:36
  20.0 6.0 %collective-permute-done.5 = bf16[256,8,128]{2,1,0:T(8,128)(2,1)S(1)} collective-permute-done((bf16[256,8,128]{2,1,0:T(8,128)(2,1)S(1)}, bf16[256,8,128]{2,1,0:T(8,128)(2,1)S(1)}, u32[]{:S(2)}, u32[]{:S(2)}) %collective-permute-start.5) | collective-permute-done | bytes 524320 | tf_op jit(solution)/shard_map/ppermute | solution.py:36
  26.0 0.3 add_convert_fusion
  26.3 0.1 dynamic-slice_select_fusion.2
  26.4 1.6 %collective-permute-start.7 = (bf16[16,4,8,128]{3,2,1,0:T(8,128)(2,1)S(1)}, bf16[16,4,8,128]{3,2,1,0:T(8,128)(2,1)S(1)}, u32[]{:S(2)}, u32[]{:S(2)}) collective-permute-start(bf16[16,4,8,128]{3,2,1,0:T(8,128)(2,1)S(1)} %get-tuple-element.44), channel_id=1, source_target_pairs={{0,128},{16,48},{1,129},{17,49},{2,130},{18,50},{3,131},{19,51},{4... | collective-permute-start | bytes 393224 | tf_op jit(solution)/shard_map/ppermute | solution.py:36
  28.0 1.3 %collective-permute-start.9 = (bf16[16,4,8,128]{3,2,1,0:T(8,128)(2,1)S(1)}, bf16[16,4,8,128]{3,2,1,0:T(8,128)(2,1)S(1)}, u32[]{:S(2)}, u32[]{:S(2)}) collective-permute-start(bf16[16,4,8,128]{3,2,1,0:T(8,128)(2,1)S(1)} %get-tuple-element.45), channel_id=1, source_target_pairs={{0,8},{16,80},{1,9},{17,81},{2,10},{18,82},{3,11},{19,83},{4,12},{... | collective-permute-start | bytes 393224 | tf_op jit(solution)/shard_map/ppermute | solution.py:36
  29.3 0.8 dynamic-slice_bitcast_fusion
  30.0 0.2 collective-permute-done.7
  30.3 4.1 %collective-permute-done.8 = bf16[16,4,8,128]{3,2,1,0:T(8,128)(2,1)S(1)} collective-permute-done((bf16[16,4,8,128]{3,2,1,0:T(8,128)(2,1)S(1)}, bf16[16,4,8,128]{3,2,1,0:T(8,128)(2,1)S(1)}, u32[]{:S(2)}, u32[]{:S(2)}) %collective-permute-start.8) | collective-permute-done | bytes 131104 | tf_op jit(solution)/shard_map/ppermute | solution.py:36
  34.4 0.1 add_convert_fusion.5
  34.5 14.8 %all_to_all.10 = bf16[8,2,4,8,128]{4,3,2,1,0:T(8,128)(2,1)S(1)} all-to-all(bf16[8,2,4,8,128]{4,3,2,1,0:T(8,128)(2,1)S(1)} %bitcast.222), channel_id=1, replica_groups={{0,1,2,3,4,5,6,7},{8,9,10,11,12,13,14,15},{16,17,18,19,20,21,22,23},{24..., dimensions={0} | all-to-all | bytes 262144 | tf_op jit(solution)/shard_map/all_to_all | solution.py:137
  49.3 0.1 fusion.33
  49.3 5.3 %collective-permute-start.10 = (bf16[2,4,8,128]{3,2,1,0:T(8,128)(2,1)S(1)}, bf16[2,4,8,128]{3,2,1,0:T(8,128)(2,1)S(1)}, u32[]{:S(2)}, u32[]{:S(2)}) collective-permute-start(bf16[2,4,8,128]{3,2,1,0:T(8,128)(2,1)S(1)} %get-tuple-element.37), channel_id=1, source_target_pairs={{0,16},{16,0},{1,17},{17,1},{2,18},{18,2},{3,19},{19,3},{4,20},{20... | collective-permute-start | bytes 49160 | tf_op jit(solution)/shard_map/ppermute | solution.py:36
  54.6 0.8 collective-permute-done.10
  55.5 0.3 collective-permute-start.11
  56.0 0.7 broadcast_in_dim.31
  56.7 3.4 %all-to-all-start.1 = ((bf16[8,2,4,8,128]{4,3,2,1,0:T(8,128)(2,1)}), bf16[8,2,4,8,128]{4,3,2,1,0:T(8,128)(2,1)S(1)}, u32[]{:S(2)}, u32[]{:S(2)}) async-start(bf16[8,2,4,8,128]{4,3,2,1,0:T(8,128)(2,1)} %broadcast_in_dim.31), calls=%async_computation.1 | async-start | bytes 262144 | tf_op jit(solution)/shard_map/all_to_all | solution.py:142
  60.1 0.6 collective-permute-start.12
  60.7 1.1 %collective-permute-start.13 = (bf16[2,2,2,4,8,128]{5,4,3,2,1,0:T(8,128)(2,1)S(1)}, bf16[2,2,2,4,8,128]{5,4,3,2,1,0:T(8,128)(2,1)S(1)}, u32[]{:S(2)}, u32[]{:S(2)}) collective-permute-start(bf16[2,2,2,4,8,128]{5,4,3,2,1,0:T(8,128)(2,1)S(1)} %pad_maximum_fusion.1), channel_id=1, source_target_pairs={{0,96},{16,112},{1,97},{17,113},{2,98},{18,114},{3,99},{19,115},{4... | collective-permute-start | bytes 196616 | tf_op jit(solution)/shard_map/ppermute | solution.py:36
  61.8 1.2 %collective-permute-start.14 = (bf16[2,2,2,4,8,128]{5,4,3,2,1,0:T(8,128)(2,1)S(1)}, bf16[2,2,2,4,8,128]{5,4,3,2,1,0:T(8,128)(2,1)S(1)}, u32[]{:S(2)}, u32[]{:S(2)}) collective-permute-start(bf16[2,2,2,4,8,128]{5,4,3,2,1,0:T(8,128)(2,1)S(1)} %pad_maximum_fusion.1), channel_id=1, source_target_pairs={{0,64},{16,80},{1,65},{17,81},{2,66},{18,82},{3,67},{19,83},{4,68}... | collective-permute-start | bytes 196616 | tf_op jit(solution)/shard_map/ppermute | solution.py:36
  63.0 0.6 bitcast_dynamic-update-slice_fusion.7
  63.6 0.6 bitcast_dynamic-update-slice_fusion.6
  64.3 0.9 collective-permute-done.13
  65.1 0.6 bitcast_dynamic-update-slice_fusion.5
  65.8 1.1 %collective-permute-done.14 = bf16[2,2,2,4,8,128]{5,4,3,2,1,0:T(8,128)(2,1)S(1)} collective-permute-done((bf16[2,2,2,4,8,128]{5,4,3,2,1,0:T(8,128)(2,1)S(1)}, bf16[2,2,2,4,8,128]{5,4,3,2,1,0:T(8,128)(2,1)S(1)}, u32[]{:S(2)}, u32[]{:S(2)}) %collective-permute-start.14) | collective-permute-done | bytes 65568 | tf_op jit(solution)/shard_map/ppermute | solution.py:36
  66.9 0.6 bitcast_dynamic-update-slice_fusion.4
  67.5 0.6 all-to-all-done.1
  68.1 0.5 collective-permute-start.15
  68.6 1.2 %slice_bitcast_fusion.17 = (bf16[2,4,2,4,8,128]{5,4,3,0,2,1:T(8,128)(2,1)S(1)}, bf16[2,2,4,4,8,128]{5,4,3,0,1,2:T(8,128)(2,1)S(1)}) fusion(bf16[4,2,2,2,4,8,128]{6,5,4,3,2,1,0:T(8,128)(2,1)} %bitcast_dynamic-update-slice_fusion.4), kind=kLoop, calls=%fused_computation.59 | loop fusion | bytes 524288 | tf_op jit(solution)/shard_map/transpose | solution.py:167
  69.9 1.1 %collective-permute-start.16 = (bf16[16,4,8,128]{3,2,1,0:T(8,128)(2,1)S(1)}, bf16[16,4,8,128]{3,2,1,0:T(8,128)(2,1)S(1)}, u32[]{:S(2)}, u32[]{:S(2)}) collective-permute-start(bf16[16,4,8,128]{3,2,1,0:T(8,128)(2,1)S(1)} %bitcast.219), channel_id=1, source_target_pairs={{0,136},{16,112},{1,137},{17,113},{2,138},{18,114},{3,139},{19,115... | collective-permute-start | bytes 393224 | tf_op jit(solution)/shard_map/ppermute | solution.py:36
  71.0 1.2 %collective-permute-start.17 = (bf16[16,4,8,128]{3,2,1,0:T(8,128)(2,1)S(1)}, bf16[16,4,8,128]{3,2,1,0:T(8,128)(2,1)S(1)}, u32[]{:S(2)}, u32[]{:S(2)}) collective-permute-start(bf16[16,4,8,128]{3,2,1,0:T(8,128)(2,1)S(1)} %bitcast.220), channel_id=1, source_target_pairs={{0,8},{16,80},{1,9},{17,81},{2,10},{18,82},{3,11},{19,83},{4,12},{... | collective-permute-start | bytes 393224 | tf_op jit(solution)/shard_map/ppermute | solution.py:36
  72.2 3.1 %collective-permute-done.16 = bf16[16,4,8,128]{3,2,1,0:T(8,128)(2,1)S(1)} collective-permute-done((bf16[16,4,8,128]{3,2,1,0:T(8,128)(2,1)S(1)}, bf16[16,4,8,128]{3,2,1,0:T(8,128)(2,1)S(1)}, u32[]{:S(2)}, u32[]{:S(2)}) %collective-permute-start.16) | collective-permute-done | bytes 131104 | tf_op jit(solution)/shard_map/ppermute | solution.py:36
  75.3 1.1 %collective-permute-done.17 = bf16[16,4,8,128]{3,2,1,0:T(8,128)(2,1)S(1)} collective-permute-done((bf16[16,4,8,128]{3,2,1,0:T(8,128)(2,1)S(1)}, bf16[16,4,8,128]{3,2,1,0:T(8,128)(2,1)S(1)}, u32[]{:S(2)}, u32[]{:S(2)}) %collective-permute-start.17) | collective-permute-done | bytes 131104 | tf_op jit(solution)/shard_map/ppermute | solution.py:36
  76.4 4.5 %collective-permute-start.18 = (bf16[2,16,8,8,128]{4,3,2,1,0:T(8,128)(2,1)S(1)}, bf16[2,16,8,8,128]{4,3,2,1,0:T(8,128)(2,1)S(1)}, u32[]{:S(2)}, u32[]{:S(2)}) collective-permute-start(bf16[2,16,8,8,128]{4,3,2,1,0:T(8,128)(2,1)S(1)} %bitcast_dynamic-update-slice_fusion), channel_id=1, source_target_pairs={{0,16},{16,0},{1,17},{17,1},{2,18},{18,2},{3,19},{19,3},{4,20},{20... | collective-permute-start | bytes 1572872 | tf_op jit(solution)/shard_map/ppermute | solution.py:36
  80.9 2.7 %collective-permute-start.21 = (bf16[2,16,8,8,128]{4,3,2,1,0:T(8,128)(2,1)S(1)}, bf16[2,16,8,8,128]{4,3,2,1,0:T(8,128)(2,1)S(1)}, u32[]{:S(2)}, u32[]{:S(2)}) collective-permute-start(bf16[2,16,8,8,128]{4,3,2,1,0:T(8,128)(2,1)S(1)} %bitcast_dynamic-update-slice_fusion), channel_id=1, source_target_pairs={{0,96},{16,152},{1,97},{17,153},{2,98},{18,154},{3,99},{19,155},{4... | collective-permute-start | bytes 1572872 | tf_op jit(solution)/shard_map/ppermute | solution.py:36
  83.6 1.5 %fusion.6 = (f32[16,8192]{1,0:T(8,128)}, f32[16,8192]{1,0:T(8,128)}, f32[16,8192]{1,0:T(8,128)}) fusion(bf16[2,32,8,128]{3,2,1,0:T(8,128)(2,1)S(1)} %bitcast.224, bf16[2,32,8,128]{3,2,1,0:T(8,128)(2,1)S(1)} %bitcast.223, f32[16,8192]{1,0:T(8,128)S(1)} %copy-done.5, f32[16,8192]{1,0:T(8,128)S(1)} %copy-done.6, f32[16,8192]{1,0:T(8,128)S(1)} %copy-done.4), kind=kLoop, calls=%fused_computation.23 | loop fusion | flops 2228224 | bytes 3407872 | tf_op jit(solution)/shard_map/reshape | solution.py:58
  85.2 10.8 %collective-permute-done.19 = bf16[2,16,8,8,128]{4,3,2,1,0:T(8,128)(2,1)S(1)} collective-permute-done((bf16[2,16,8,8,128]{4,3,2,1,0:T(8,128)(2,1)S(1)}, bf16[2,16,8,8,128]{4,3,2,1,0:T(8,128)(2,1)S(1)}, u32[]{:S(2)}, u32[]{:S(2)}) %collective-permute-start.19) | collective-permute-done | bytes 524320 | tf_op jit(solution)/shard_map/ppermute | solution.py:36
  96.0 2.1 %collective-permute-start.22 = (bf16[2,16,8,8,128]{4,3,2,1,0:T(8,128)(2,1)S(1)}, bf16[2,16,8,8,128]{4,3,2,1,0:T(8,128)(2,1)S(1)}, u32[]{:S(2)}, u32[]{:S(2)}) collective-permute-start(bf16[2,16,8,8,128]{4,3,2,1,0:T(8,128)(2,1)S(1)} %collective-permute-done.21), channel_id=1, source_target_pairs={{0,16},{16,0},{1,17},{17,1},{2,18},{18,2},{3,19},{19,3},{4,20},{20... | collective-permute-start | bytes 1572872 | tf_op jit(solution)/shard_map/ppermute | solution.py:36
  98.5 1.1 %collective-permute-done.22 = bf16[2,16,8,8,128]{4,3,2,1,0:T(8,128)(2,1)S(1)} collective-permute-done((bf16[2,16,8,8,128]{4,3,2,1,0:T(8,128)(2,1)S(1)}, bf16[2,16,8,8,128]{4,3,2,1,0:T(8,128)(2,1)S(1)}, u32[]{:S(2)}, u32[]{:S(2)}) %collective-permute-start.22) | collective-permute-done | bytes 524320 | tf_op jit(solution)/shard_map/ppermute | solution.py:36
  99.9 0.6 collective-permute-done.24
  100.5 0.0 copy-start.2
  100.5 2.0 %copy-done.2 = bf16[32,64,8,128]{3,2,1,0:T(8,128)(2,1)} copy-done((bf16[32,64,8,128]{3,2,1,0:T(8,128)(2,1)}, bf16[32,64,8,128]{3,2,1,0:T(8,128)(2,1)S(1)}, u32[]{:S(2)}) %copy-start.2) | copy-done | bytes 4194328
  (66 shorter events, 1.2 us)
Async XLA Ops:
  3.8 2.6 %collective-permute-start = (bf16[256,8,128]{2,1,0:T(8,128)(2,1)}, bf16[256,8,128]{2,1,0:T(8,128)(2,1)}, u32[]{:S(2)}, u32[]{:S(2)}) collective-permute-start(bf16[256,8,128]{2,1,0:T(8,128)(2,1)} %bitcast_select_fusion), channel_id=1, source_target_pairs={{0,16},{16,0},{1,17},{17,1},{2,18},{18,2},{3,19},{19,3},{4,20},{20... | collective-permute-start | bytes 1572872 | tf_op jit(solution)/shard_map/ppermute | solution.py:36
  6.2 2.3 %copy-start = (bf16[1,1,256,8192]{3,2,1,0:T(8,128)(2,1)S(1)}, bf16[1,1,256,8192]{3,2,1,0:T(8,128)(2,1)}, u32[]{:S(2)}) copy-start(bf16[1,1,256,8192]{3,2,1,0:T(8,128)(2,1)} %param.4) | copy-start | bytes 12582916
  9.1 4.1 %collective-permute-start.1 = (bf16[256,8,128]{2,1,0:T(8,128)(2,1)S(1)}, bf16[256,8,128]{2,1,0:T(8,128)(2,1)S(1)}, u32[]{:S(2)}, u32[]{:S(2)}) collective-permute-start(bf16[256,8,128]{2,1,0:T(8,128)(2,1)S(1)} %bitcast_select_fusion.5), channel_id=1, source_target_pairs={{0,16},{16,0},{1,17},{17,1},{2,18},{18,2},{3,19},{19,3},{4,20},{20... | collective-permute-start | bytes 1572872 | tf_op jit(solution)/shard_map/ppermute | solution.py:36
  9.3 6.5 %collective-permute-start.3 = (bf16[256,8,128]{2,1,0:T(8,128)(2,1)S(1)}, bf16[256,8,128]{2,1,0:T(8,128)(2,1)S(1)}, u32[]{:S(2)}, u32[]{:S(2)}) collective-permute-start(bf16[256,8,128]{2,1,0:T(8,128)(2,1)S(1)} %bitcast_select_fusion.1), channel_id=1, source_target_pairs={{0,16},{16,0},{1,17},{17,1},{2,18},{18,2},{3,19},{19,3},{4,20},{20... | collective-permute-start | bytes 1572872 | tf_op jit(solution)/shard_map/ppermute | solution.py:36
  10.0 3.6 %collective-permute-start.2 = (bf16[256,8,128]{2,1,0:T(8,128)(2,1)S(1)}, bf16[256,8,128]{2,1,0:T(8,128)(2,1)S(1)}, u32[]{:S(2)}, u32[]{:S(2)}) collective-permute-start(bf16[256,8,128]{2,1,0:T(8,128)(2,1)S(1)} %bitcast_select_fusion.3), channel_id=1, source_target_pairs={{0,16},{16,0},{1,17},{17,1},{2,18},{18,2},{3,19},{19,3},{4,20},{20... | collective-permute-start | bytes 1572872 | tf_op jit(solution)/shard_map/ppermute | solution.py:36
  10.1 9.9 %collective-permute-start.6 = (bf16[256,8,128]{2,1,0:T(8,128)(2,1)S(1)}, bf16[256,8,128]{2,1,0:T(8,128)(2,1)S(1)}, u32[]{:S(2)}, u32[]{:S(2)}) collective-permute-start(bf16[256,8,128]{2,1,0:T(8,128)(2,1)S(1)} %add_convert_fusion.4), channel_id=1, source_target_pairs={{0,64},{16,24},{1,65},{17,25},{2,66},{18,26},{3,67},{19,27},{4,68}... | collective-permute-start | bytes 1572872 | tf_op jit(solution)/shard_map/ppermute | solution.py:36
  13.9 15.4 %copy-start.4 = (f32[16,8192]{1,0:T(8,128)S(1)}, f32[16,8192]{1,0:T(8,128)}, u32[]{:S(2)}) copy-start(f32[16,8192]{1,0:T(8,128)} %param.5) | copy-start | bytes 1572868
  13.9 15.3 %copy-start.5 = (f32[16,8192]{1,0:T(8,128)S(1)}, f32[16,8192]{1,0:T(8,128)}, u32[]{:S(2)}) copy-start(f32[16,8192]{1,0:T(8,128)} %param.7) | copy-start | bytes 1572868
  13.9 12.1 %collective-permute-start.5 = (bf16[256,8,128]{2,1,0:T(8,128)(2,1)S(1)}, bf16[256,8,128]{2,1,0:T(8,128)(2,1)S(1)}, u32[]{:S(2)}, u32[]{:S(2)}) collective-permute-start(bf16[256,8,128]{2,1,0:T(8,128)(2,1)S(1)} %add_convert_fusion.2), channel_id=1, source_target_pairs={{0,96},{16,152},{1,97},{17,153},{2,98},{18,154},{3,99},{19,155},{4... | collective-permute-start | bytes 1572872 | tf_op jit(solution)/shard_map/ppermute | solution.py:36
  15.7 10.4 %collective-permute-start.4 = (bf16[256,8,128]{2,1,0:T(8,128)(2,1)S(1)}, bf16[256,8,128]{2,1,0:T(8,128)(2,1)S(1)}, u32[]{:S(2)}, u32[]{:S(2)}) collective-permute-start(bf16[256,8,128]{2,1,0:T(8,128)(2,1)S(1)} %add_convert_fusion.3), channel_id=1, source_target_pairs={{0,32},{16,144},{1,33},{17,145},{2,34},{18,146},{3,35},{19,147},{4... | collective-permute-start | bytes 1572872 | tf_op jit(solution)/shard_map/ppermute | solution.py:36
  26.4 3.9 %collective-permute-start.7 = (bf16[16,4,8,128]{3,2,1,0:T(8,128)(2,1)S(1)}, bf16[16,4,8,128]{3,2,1,0:T(8,128)(2,1)S(1)}, u32[]{:S(2)}, u32[]{:S(2)}) collective-permute-start(bf16[16,4,8,128]{3,2,1,0:T(8,128)(2,1)S(1)} %get-tuple-element.44), channel_id=1, source_target_pairs={{0,128},{16,48},{1,129},{17,49},{2,130},{18,50},{3,131},{19,51},{4... | collective-permute-start | bytes 393224 | tf_op jit(solution)/shard_map/ppermute | solution.py:36
  28.0 6.4 %collective-permute-start.8 = (bf16[16,4,8,128]{3,2,1,0:T(8,128)(2,1)S(1)}, bf16[16,4,8,128]{3,2,1,0:T(8,128)(2,1)S(1)}, u32[]{:S(2)}, u32[]{:S(2)}) collective-permute-start(bf16[16,4,8,128]{3,2,1,0:T(8,128)(2,1)S(1)} %get-tuple-element.46), channel_id=1, source_target_pairs={{0,136},{16,112},{1,137},{17,113},{2,138},{18,114},{3,139},{19,115... | collective-permute-start | bytes 393224 | tf_op jit(solution)/shard_map/ppermute | solution.py:36
  28.0 6.4 %collective-permute-start.9 = (bf16[16,4,8,128]{3,2,1,0:T(8,128)(2,1)S(1)}, bf16[16,4,8,128]{3,2,1,0:T(8,128)(2,1)S(1)}, u32[]{:S(2)}, u32[]{:S(2)}) collective-permute-start(bf16[16,4,8,128]{3,2,1,0:T(8,128)(2,1)S(1)} %get-tuple-element.45), channel_id=1, source_target_pairs={{0,8},{16,80},{1,9},{17,81},{2,10},{18,82},{3,11},{19,83},{4,12},{... | collective-permute-start | bytes 393224 | tf_op jit(solution)/shard_map/ppermute | solution.py:36
  49.3 6.1 %collective-permute-start.10 = (bf16[2,4,8,128]{3,2,1,0:T(8,128)(2,1)S(1)}, bf16[2,4,8,128]{3,2,1,0:T(8,128)(2,1)S(1)}, u32[]{:S(2)}, u32[]{:S(2)}) collective-permute-start(bf16[2,4,8,128]{3,2,1,0:T(8,128)(2,1)S(1)} %get-tuple-element.37), channel_id=1, source_target_pairs={{0,16},{16,0},{1,17},{17,1},{2,18},{18,2},{3,19},{19,3},{4,20},{20... | collective-permute-start | bytes 49160 | tf_op jit(solution)/shard_map/ppermute | solution.py:36
  55.5 4.5 %collective-permute-start.11 = (bf16[2,2,4,8,128]{4,3,2,1,0:T(8,128)(2,1)S(1)}, bf16[2,2,4,8,128]{4,3,2,1,0:T(8,128)(2,1)S(1)}, u32[]{:S(2)}, u32[]{:S(2)}) collective-permute-start(bf16[2,2,4,8,128]{4,3,2,1,0:T(8,128)(2,1)S(1)} %pad_maximum_fusion.2), channel_id=1, source_target_pairs={{0,128},{16,144},{1,129},{17,145},{2,130},{18,146},{3,131},{19,147... | collective-permute-start | bytes 98312 | tf_op jit(solution)/shard_map/ppermute | solution.py:36
  55.8 27.7 %copy-start.6 = (f32[16,8192]{1,0:T(8,128)S(1)}, f32[16,8192]{1,0:T(8,128)}, u32[]{:S(2)}) copy-start(f32[16,8192]{1,0:T(8,128)} %param.6) | copy-start | bytes 1572868
  55.8 16.3 %copy-start.3 = (bf16[2,16,8,8,128]{4,3,2,1,0:T(8,128)(2,1)S(1)}, bf16[2,16,8,8,128]{4,3,2,1,0:T(8,128)(2,1)}, u32[]{:S(2)}) copy-start(bf16[2,16,8,8,128]{4,3,2,1,0:T(8,128)(2,1)} %shard_map.77) | copy-start | bytes 1572868
  56.7 11.4 %all-to-all-start.1 = ((bf16[8,2,4,8,128]{4,3,2,1,0:T(8,128)(2,1)}), bf16[8,2,4,8,128]{4,3,2,1,0:T(8,128)(2,1)S(1)}, u32[]{:S(2)}, u32[]{:S(2)}) async-start(bf16[8,2,4,8,128]{4,3,2,1,0:T(8,128)(2,1)} %broadcast_in_dim.31), calls=%async_computation.1 | async-start | bytes 262144 | tf_op jit(solution)/shard_map/all_to_all | solution.py:142
  60.1 3.6 %collective-permute-start.12 = (bf16[2,2,2,4,8,128]{5,4,3,2,1,0:T(8,128)(2,1)S(1)}, bf16[2,2,2,4,8,128]{5,4,3,2,1,0:T(8,128)(2,1)S(1)}, u32[]{:S(2)}, u32[]{:S(2)}) collective-permute-start(bf16[2,2,2,4,8,128]{5,4,3,2,1,0:T(8,128)(2,1)S(1)} %pad_maximum_fusion.1), channel_id=1, source_target_pairs={{0,32},{16,48},{1,33},{17,49},{2,34},{18,50},{3,35},{19,51},{4,36}... | collective-permute-start | bytes 196616 | tf_op jit(solution)/shard_map/ppermute | solution.py:36
  60.7 4.5 %collective-permute-start.13 = (bf16[2,2,2,4,8,128]{5,4,3,2,1,0:T(8,128)(2,1)S(1)}, bf16[2,2,2,4,8,128]{5,4,3,2,1,0:T(8,128)(2,1)S(1)}, u32[]{:S(2)}, u32[]{:S(2)}) collective-permute-start(bf16[2,2,2,4,8,128]{5,4,3,2,1,0:T(8,128)(2,1)S(1)} %pad_maximum_fusion.1), channel_id=1, source_target_pairs={{0,96},{16,112},{1,97},{17,113},{2,98},{18,114},{3,99},{19,115},{4... | collective-permute-start | bytes 196616 | tf_op jit(solution)/shard_map/ppermute | solution.py:36
  61.8 5.1 %collective-permute-start.14 = (bf16[2,2,2,4,8,128]{5,4,3,2,1,0:T(8,128)(2,1)S(1)}, bf16[2,2,2,4,8,128]{5,4,3,2,1,0:T(8,128)(2,1)S(1)}, u32[]{:S(2)}, u32[]{:S(2)}) collective-permute-start(bf16[2,2,2,4,8,128]{5,4,3,2,1,0:T(8,128)(2,1)S(1)} %pad_maximum_fusion.1), channel_id=1, source_target_pairs={{0,64},{16,80},{1,65},{17,81},{2,66},{18,82},{3,67},{19,83},{4,68}... | collective-permute-start | bytes 196616 | tf_op jit(solution)/shard_map/ppermute | solution.py:36
  68.1 17.0 %copy-start.1 = (bf16[32,64,8,128]{3,2,1,0:T(8,128)(2,1)S(1)}, bf16[32,64,8,128]{3,2,1,0:T(8,128)(2,1)}, u32[]{:S(2)}) copy-start(bf16[32,64,8,128]{3,2,1,0:T(8,128)(2,1)} %shard_map.76) | copy-start | bytes 12582916
  68.1 4.1 %collective-permute-start.15 = (bf16[16,4,8,128]{3,2,1,0:T(8,128)(2,1)S(1)}, bf16[16,4,8,128]{3,2,1,0:T(8,128)(2,1)S(1)}, u32[]{:S(2)}, u32[]{:S(2)}) collective-permute-start(bf16[16,4,8,128]{3,2,1,0:T(8,128)(2,1)S(1)} %bitcast.218), channel_id=1, source_target_pairs={{0,128},{16,48},{1,129},{17,49},{2,130},{18,50},{3,131},{19,51},{4... | collective-permute-start | bytes 393224 | tf_op jit(solution)/shard_map/ppermute | solution.py:36
  69.9 5.4 %collective-permute-start.16 = (bf16[16,4,8,128]{3,2,1,0:T(8,128)(2,1)S(1)}, bf16[16,4,8,128]{3,2,1,0:T(8,128)(2,1)S(1)}, u32[]{:S(2)}, u32[]{:S(2)}) collective-permute-start(bf16[16,4,8,128]{3,2,1,0:T(8,128)(2,1)S(1)} %bitcast.219), channel_id=1, source_target_pairs={{0,136},{16,112},{1,137},{17,113},{2,138},{18,114},{3,139},{19,115... | collective-permute-start | bytes 393224 | tf_op jit(solution)/shard_map/ppermute | solution.py:36
  71.0 5.4 %collective-permute-start.17 = (bf16[16,4,8,128]{3,2,1,0:T(8,128)(2,1)S(1)}, bf16[16,4,8,128]{3,2,1,0:T(8,128)(2,1)S(1)}, u32[]{:S(2)}, u32[]{:S(2)}) collective-permute-start(bf16[16,4,8,128]{3,2,1,0:T(8,128)(2,1)S(1)} %bitcast.220), channel_id=1, source_target_pairs={{0,8},{16,80},{1,9},{17,81},{2,10},{18,82},{3,11},{19,83},{4,12},{... | collective-permute-start | bytes 393224 | tf_op jit(solution)/shard_map/ppermute | solution.py:36
  76.4 21.7 %collective-permute-start.18 = (bf16[2,16,8,8,128]{4,3,2,1,0:T(8,128)(2,1)S(1)}, bf16[2,16,8,8,128]{4,3,2,1,0:T(8,128)(2,1)S(1)}, u32[]{:S(2)}, u32[]{:S(2)}) collective-permute-start(bf16[2,16,8,8,128]{4,3,2,1,0:T(8,128)(2,1)S(1)} %bitcast_dynamic-update-slice_fusion), channel_id=1, source_target_pairs={{0,16},{16,0},{1,17},{17,1},{2,18},{18,2},{3,19},{19,3},{4,20},{20... | collective-permute-start | bytes 1572872 | tf_op jit(solution)/shard_map/ppermute | solution.py:36
  80.9 15.2 %collective-permute-start.19 = (bf16[2,16,8,8,128]{4,3,2,1,0:T(8,128)(2,1)S(1)}, bf16[2,16,8,8,128]{4,3,2,1,0:T(8,128)(2,1)S(1)}, u32[]{:S(2)}, u32[]{:S(2)}) collective-permute-start(bf16[2,16,8,8,128]{4,3,2,1,0:T(8,128)(2,1)S(1)} %bitcast_dynamic-update-slice_fusion), channel_id=1, source_target_pairs={{0,32},{16,144},{1,33},{17,145},{2,34},{18,146},{3,35},{19,147},{4... | collective-permute-start | bytes 1572872 | tf_op jit(solution)/shard_map/ppermute | solution.py:36
  80.9 15.2 %collective-permute-start.21 = (bf16[2,16,8,8,128]{4,3,2,1,0:T(8,128)(2,1)S(1)}, bf16[2,16,8,8,128]{4,3,2,1,0:T(8,128)(2,1)S(1)}, u32[]{:S(2)}, u32[]{:S(2)}) collective-permute-start(bf16[2,16,8,8,128]{4,3,2,1,0:T(8,128)(2,1)S(1)} %bitcast_dynamic-update-slice_fusion), channel_id=1, source_target_pairs={{0,96},{16,152},{1,97},{17,153},{2,98},{18,154},{3,99},{19,155},{4... | collective-permute-start | bytes 1572872 | tf_op jit(solution)/shard_map/ppermute | solution.py:36
  83.6 14.6 %collective-permute-start.23 = (bf16[2,16,8,8,128]{4,3,2,1,0:T(8,128)(2,1)S(1)}, bf16[2,16,8,8,128]{4,3,2,1,0:T(8,128)(2,1)S(1)}, u32[]{:S(2)}, u32[]{:S(2)}) collective-permute-start(bf16[2,16,8,8,128]{4,3,2,1,0:T(8,128)(2,1)S(1)} %bitcast_dynamic-update-slice_fusion), channel_id=1, source_target_pairs={{0,64},{16,24},{1,65},{17,25},{2,66},{18,26},{3,67},{19,27},{4,68}... | collective-permute-start | bytes 1572872 | tf_op jit(solution)/shard_map/ppermute | solution.py:36
  96.0 2.3 %collective-permute-start.20 = (bf16[2,16,8,8,128]{4,3,2,1,0:T(8,128)(2,1)S(1)}, bf16[2,16,8,8,128]{4,3,2,1,0:T(8,128)(2,1)S(1)}, u32[]{:S(2)}, u32[]{:S(2)}) collective-permute-start(bf16[2,16,8,8,128]{4,3,2,1,0:T(8,128)(2,1)S(1)} %collective-permute-done.19), channel_id=1, source_target_pairs={{0,16},{16,0},{1,17},{17,1},{2,18},{18,2},{3,19},{19,3},{4,20},{20... | collective-permute-start | bytes 1572872 | tf_op jit(solution)/shard_map/ppermute | solution.py:36
  96.0 3.6 %collective-permute-start.22 = (bf16[2,16,8,8,128]{4,3,2,1,0:T(8,128)(2,1)S(1)}, bf16[2,16,8,8,128]{4,3,2,1,0:T(8,128)(2,1)S(1)}, u32[]{:S(2)}, u32[]{:S(2)}) collective-permute-start(bf16[2,16,8,8,128]{4,3,2,1,0:T(8,128)(2,1)S(1)} %collective-permute-done.21), channel_id=1, source_target_pairs={{0,16},{16,0},{1,17},{17,1},{2,18},{18,2},{3,19},{19,3},{4,20},{20... | collective-permute-start | bytes 1572872 | tf_op jit(solution)/shard_map/ppermute | solution.py:36
  98.1 2.3 %collective-permute-start.24 = (bf16[2,16,8,8,128]{4,3,2,1,0:T(8,128)(2,1)S(1)}, bf16[2,16,8,8,128]{4,3,2,1,0:T(8,128)(2,1)S(1)}, u32[]{:S(2)}, u32[]{:S(2)}) collective-permute-start(bf16[2,16,8,8,128]{4,3,2,1,0:T(8,128)(2,1)S(1)} %collective-permute-done.23), channel_id=1, source_target_pairs={{0,16},{16,0},{1,17},{17,1},{2,18},{18,2},{3,19},{19,3},{4,20},{20... | collective-permute-start | bytes 1572872 | tf_op jit(solution)/shard_map/ppermute | solution.py:36
  100.5 2.0 %copy-start.2 = (bf16[32,64,8,128]{3,2,1,0:T(8,128)(2,1)}, bf16[32,64,8,128]{3,2,1,0:T(8,128)(2,1)S(1)}, u32[]{:S(2)}) copy-start(bf16[32,64,8,128]{3,2,1,0:T(8,128)(2,1)S(1)} %fusion.7) | copy-start | bytes 12582916
